TPU v7x, 32 devices: a whole 2x2x4 slice. The times are simulated.
32 devices in a mesh: outer: 4 (over y, core), inner: 2 (over x), region: 4 (over z).
Axes of the slice: x: 2, y: 2, z: 4, core: 2. Of those that a mesh axis runs over, the one named last changes fastest.
Arguments:
- observations: float32 [64, 128], P(('region', 'outer', 'inner')), parts along dimension 0, may hold values from -6 to 6
- obs_mask: int32 [64, 128], P(('region', 'outer', 'inner')), parts along dimension 0, may hold values 0 or 1
- sensor_map: int32 [512], P('region'), parts along dimension 0, may hold values from 0 to 127
- transition: float32 [128, 128], replicated, may hold values from -1 to 1
- proc_noise: float32 [128, 128], replicated, may hold values from -1 to 1, as said below
- obs_var: float32 [128], replicated, may hold values from 0.1 to 1
- prior_mean: float32 [512], P('region'), parts along dimension 0, may hold values from -6 to 6
- prior_var: float32 [512], P('region'), parts along dimension 0, may hold values from 0.5 to 4
Outputs:
- filt_mean: float32 [64, 128], P(('region', 'outer', 'inner')), parts along dimension 0
- filt_cov: float32 [64, 128, 128], P(('region', 'outer', 'inner')), parts along dimension 0
There are 4 independent parts, one for each index of `region`. A program takes and returns all parts, laid end to end along the dimension named above; an argument that names none is the same for every part. Nothing has to cross between parts.
Inputs may be any that keep to these rules, and one draw needn't show every extreme that they name: `proc_noise`: symmetric positive definite.
All inputs are finite; a program needn't handle non-finite values. No bound on the sum of `obs_mask` on one device may be relied on, other than what follows from the above.
Results may differ from a plain program's by a relative error of at most 0.00017.
Values sent between devices are 32-bit elements; how exact they have to be, the bound alone decides.
No kernel may reach another device: no remote copies, remote signals or barrier semaphores. Data moves between devices by JAX's collectives and lax.ppermute only.
A program may use at most 128 MiB of HBM per device.

v0:
```python
import jax
import jax.numpy as jnp
from jax import lax
from jax.sharding import PartitionSpec as P


def entering(part, axis, combine, identity):
    place = lax.axis_index(axis)
    gathered = jax.tree.map(lambda a: lax.all_gather(a, axis), part)
    state = jax.tree.map(lambda a, e: jnp.zeros_like(a) + jnp.asarray(e, a.dtype), part, identity)

    def one(hop, state):
        return combine(
            state, jax.tree.map(lambda a: lax.dynamic_index_in_dim(a, hop, 0, False), gathered)
        )

    return lax.fori_loop(0, place, one, state)


def from_root(value, axis, source):
    kept = jnp.where(lax.axis_index(axis) == source, value, 0).astype(value.dtype)
    return lax.psum(kept, axis)


def highest(left, right):
    return jnp.dot(left, right, precision=lax.Precision.HIGHEST)


def filter_step(carried, inputs, transition, proc_noise, sensor_map, obs_var):
    prev_mean, prev_cov = carried
    observed, mask_row = inputs
    weights = mask_row.astype(jnp.float32)
    pred_mean = highest(transition, prev_mean)
    pred_cov = highest(highest(transition, prev_cov), transition.T) + proc_noise
    picked = pred_cov[sensor_map] * weights[:, None]
    innov_cov = picked[:, sensor_map] * weights[None, :] + jnp.diag(obs_var)
    factor = jnp.linalg.cholesky(innov_cov)
    solved = jax.scipy.linalg.cho_solve((factor, True), picked)
    innovation = weights * (observed - pred_mean[sensor_map])
    new_mean = pred_mean + highest(solved.T, innovation)
    new_cov = pred_cov - highest(picked.T, solved)
    new_cov = 0.5 * (new_cov + new_cov.T)
    return ((new_mean, new_cov), (new_mean, new_cov))


def step_element(transition, proc_noise, sensor_map, obs_var, observed, mask_row):
    weights = mask_row.astype(jnp.float32)
    noise_rows = proc_noise[sensor_map] * weights[:, None]
    trans_rows = transition[sensor_map] * weights[:, None]
    innov_cov = noise_rows[:, sensor_map] * weights[None, :] + jnp.diag(obs_var)
    factor = jnp.linalg.cholesky(innov_cov)
    solved = jax.scipy.linalg.cho_solve((factor, True), noise_rows)
    masked_obs = weights * observed
    jump = transition - highest(solved.T, trans_rows)
    spread = proc_noise - highest(noise_rows.T, solved)
    spread = 0.5 * (spread + spread.T)
    offset = highest(solved.T, masked_obs)
    whitened = jax.scipy.linalg.solve_triangular(factor, trans_rows, lower=True)
    white_obs = jax.scipy.linalg.solve_triangular(factor, masked_obs, lower=True)
    info_vec = highest(whitened.T, white_obs)
    info_mat = highest(whitened.T, whitened)
    return (
        jnp.stack([jump, spread, info_mat]),
        jnp.stack([offset, info_vec]),
        jnp.ones((), jnp.float32),
    )


def first_element(
    transition, proc_noise, sensor_map, obs_var, prior_mean, prior_var, observed, mask_row
):
    start_state = (prior_mean, jnp.diag(prior_var))
    new_state, dropped = filter_step(
        start_state, (observed, mask_row), transition, proc_noise, sensor_map, obs_var
    )
    zero_mat = jnp.zeros_like(transition)
    zero_vec = jnp.zeros_like(prior_mean)
    return (
        jnp.stack([zero_mat, new_state[1], zero_mat]),
        jnp.stack([new_state[0], zero_vec]),
        jnp.ones((), jnp.float32),
    )


def blend_parts(early_spread, early_live, late_info):
    ident_mat = jnp.eye(early_spread.shape[0], dtype=jnp.float32)
    spread_root = jnp.linalg.cholesky(early_spread + (1.0 - early_live) * ident_mat)
    core = ident_mat + highest(spread_root.T, highest(late_info, spread_root))
    core = 0.5 * (core + core.T)
    core_root = jnp.linalg.cholesky(core)
    reduced = jax.scipy.linalg.solve_triangular(core_root, spread_root.T, lower=True)
    blended = highest(reduced.T, reduced)
    return (ident_mat, blended)


def combine(earlier, later):
    early_mats, early_vecs, early_live = earlier
    late_mats, late_vecs, late_live = later
    early_jump, early_spread, early_info = (early_mats[0], early_mats[1], early_mats[2])
    late_jump, late_spread, late_info = (late_mats[0], late_mats[1], late_mats[2])
    early_offset, early_vec = (early_vecs[0], early_vecs[1])
    late_offset, late_vec = (late_vecs[0], late_vecs[1])
    ident_mat, blended = blend_parts(early_spread, early_live, late_info)
    correction = ident_mat - highest(blended, late_info)
    moved = highest(correction, early_jump)
    jump = highest(late_jump, moved)
    offset = (
        highest(late_jump, highest(correction, early_offset) + highest(blended, late_vec))
        + late_offset
    )
    spread = highest(highest(late_jump, blended), late_jump.T) + late_spread
    spread = 0.5 * (spread + spread.T)
    info_mat = highest(moved.T, highest(late_info, early_jump)) + early_info
    info_mat = 0.5 * (info_mat + info_mat.T)
    info_vec = (
        highest(early_jump.T, highest(correction.T, late_vec - highest(late_info, early_offset)))
        + early_vec
    )
    joined = (
        jnp.stack([jump, spread, info_mat]),
        jnp.stack([offset, info_vec]),
        jnp.maximum(early_live, late_live),
    )
    keep_late = jax.tree.map(
        lambda joined_leaf, other_leaf: jnp.where(late_live > 0.5, joined_leaf, other_leaf),
        joined,
        earlier,
    )
    return jax.tree.map(
        lambda joined_leaf, other_leaf: jnp.where(early_live > 0.5, joined_leaf, other_leaf),
        keep_late,
        later,
    )


def place_state(state_el, element, prior_mean, prior_cov):
    state_mats, state_vecs, state_live = state_el
    elem_mats, elem_vecs, elem_live = element
    late_jump, late_spread, late_info = (elem_mats[0], elem_mats[1], elem_mats[2])
    late_offset, late_vec = (elem_vecs[0], elem_vecs[1])
    early_spread = state_mats[1]
    early_offset = state_vecs[0]
    ident_mat, blended = blend_parts(early_spread, state_live, late_info)
    shifted = early_offset - highest(blended, highest(late_info, early_offset))
    mean_new = highest(late_jump, shifted + highest(blended, late_vec)) + late_offset
    cov_new = highest(highest(late_jump, blended), late_jump.T) + late_spread
    cov_new = 0.5 * (cov_new + cov_new.T)
    mean_pick = jnp.where(
        state_live > 0.5,
        jnp.where(elem_live > 0.5, mean_new, early_offset),
        jnp.where(elem_live > 0.5, late_offset, prior_mean),
    )
    cov_pick = jnp.where(
        state_live > 0.5,
        jnp.where(elem_live > 0.5, cov_new, early_spread),
        jnp.where(elem_live > 0.5, late_spread, prior_cov),
    )
    return (mean_pick, cov_pick)


def local(
    observations, obs_mask, sensor_map, transition, proc_noise, obs_var, prior_mean, prior_var
):
    steps_here = observations.shape[0]
    state_dim = transition.shape[0]
    position = lax.axis_index("outer") * lax.axis_size("inner") + lax.axis_index("inner")

    def generic_at(counter):
        observed = lax.dynamic_index_in_dim(observations, counter, 0, keepdims=False)
        mask_row = lax.dynamic_index_in_dim(obs_mask, counter, 0, keepdims=False)
        return step_element(transition, proc_noise, sensor_map, obs_var, observed, mask_row)

    first_piece = lax.cond(
        position == 0,
        lambda: first_element(
            transition,
            proc_noise,
            sensor_map,
            obs_var,
            prior_mean,
            prior_var,
            observations[0],
            obs_mask[0],
        ),
        lambda: generic_at(0),
    )

    def fold_step(counter, carried):
        return combine(carried, generic_at(counter))

    own_element = lax.fori_loop(1, steps_here, fold_step, first_piece)
    zero_mat = jnp.zeros((state_dim, state_dim), jnp.float32)
    identity_el = (
        jnp.stack([jnp.eye(state_dim, dtype=jnp.float32), zero_mat, zero_mat]),
        jnp.zeros((2, state_dim), jnp.float32),
        jnp.zeros((), jnp.float32),
    )
    prior_cov = jnp.diag(prior_var)
    within = entering(own_element, "inner", combine, identity_el)
    through = combine(within, own_element)
    group_whole = jax.tree.map(
        lambda part: from_root(part, "inner", lax.axis_size("inner") - 1), through
    )
    before = entering(group_whole, "outer", combine, identity_el)
    start_mean, start_cov = place_state(before, within, prior_mean, prior_cov)

    def advance(carried, inputs):
        return filter_step(carried, inputs, transition, proc_noise, sensor_map, obs_var)

    last_state, outputs = lax.scan(advance, (start_mean, start_cov), (observations, obs_mask))
    return (outputs[0], outputs[1])


def solution(mesh):
    return jax.shard_map(
        local,
        mesh=mesh,
        in_specs=(
            P(("region", "outer", "inner"), None),
            P(("region", "outer", "inner"), None),
            P("region"),
            P(),
            P(),
            P(),
            P("region"),
            P("region"),
        ),
        out_specs=(
            P(("region", "outer", "inner"), None),
            P(("region", "outer", "inner"), None, None),
        ),
        check_vma=False,
    )
```

profile of v0, /device:TPU:31, one launch (start us, length us, event | category | flops | bytes accessed | tf_op | source)
XLA Modules:
  0.0 488.2 jit_solution(18340099609839349702)
XLA Ops:
  11.5 33.8 %conditional.1 = (f32[3,128,128]{2,1,0:T(8,128)S(1)}, f32[]{:T(128)}, f32[128]{0:T(128)S(1)}, f32[128]{0:T(128)S(1)}) conditional(s32[]{:T(128)} %convert_element_type.141, (s32[128]{0:T(128)S(1)}, f32[128,128]{1,0:T(8,128)S(1)}, s32[2,128]{1,0:T(2,128)S(1)}, f32[128]{0:T(128)S(1)}, f32[128,128]{1,0:T(8,128)S(1)}, ...), branch_computations={%region_0.7_spmd, %region_3.8_spmd} | conditional | flops 152078464 | bytes 3883050 | solution.py:173
  13.2 11.7 %custom-call.40 = f32[128,128]{1,0:T(8,128)S(1)} custom-call(f32[128,128]{1,0:T(8,128)S(1)} %fusion.150), custom_call_target="Cholesky" | custom-call | tf_op jit(solution)/shard_map/cond/branch_0_fun/jit(cholesky)/cholesky/custom-call.1 | solution.py:51
  26.2 9.8 %custom-call.41 = f32[1,128,128]{1,2,0:T(8,128)S(1)} custom-call(f32[1,128,128]{2,1,0:T(8,128)S(1)} %fusion.137), custom_call_target="InvertDiagBlocksLowerTriangular" | custom-call | tf_op jit(solution)/shard_map/cond/branch_0_fun/jit(_cho_solve)/triangular_solve | solution.py:52
  46.7 11.7 %custom-call.60 = f32[128,128]{1,0:T(8,128)S(1)} custom-call(f32[128,128]{1,0:T(8,128)S(1)} %copy.232), custom_call_target="Cholesky" | custom-call | tf_op jit(solution)/shard_map/while/body/eval_jaxpr/jit(cholesky)/cholesky/custom-call.1 | solution.py:51
  59.7 9.8 %custom-call.61 = f32[1,128,128]{1,2,0:T(8,128)S(1)} custom-call(f32[1,128,128]{2,1,0:T(8,128)S(1)} %fusion.222), custom_call_target="InvertDiagBlocksLowerTriangular" | custom-call | tf_op jit(solution)/shard_map/while/body/eval_jaxpr/jit(_cho_solve)/triangular_solve | solution.py:52
  77.7 11.7 %custom-call.63 = f32[128,128]{1,0:T(8,128)S(1)} custom-call(f32[128,128]{1,0:T(8,128)S(1)} %copy.237), custom_call_target="Cholesky" | custom-call | tf_op jit(solution)/shard_map/while/body/eval_jaxpr/jit(cholesky)/cholesky/custom-call.1 | solution.py:87
  92.1 11.7 %custom-call.65 = f32[128,128]{1,0:T(8,128)S(1)} custom-call(f32[128,128]{1,0:T(8,128)S(1)} %copy.239), custom_call_target="Cholesky" | custom-call | tf_op jit(solution)/shard_map/while/body/eval_jaxpr/jit(cholesky)/cholesky/custom-call.1 | solution.py:90
  105.2 9.8 %custom-call.66 = f32[1,128,128]{1,2,0:T(8,128)S(1)} custom-call(f32[1,128,128]{2,1,0:T(8,128)S(1)} %fusion.223), custom_call_target="InvertDiagBlocksLowerTriangular" | custom-call | tf_op jit(solution)/shard_map/while/body/eval_jaxpr/jit(_solve_triangular)/triangular_solve/custom-call.0 | solution.py:91
  128.2 44.9 %while.55 = (s32[]{:T(128)}, f32[3,128,128]{2,1,0:T(8,128)S(1)}, f32[2,128]{1,0:T(2,128)S(1)}, f32[]{:T(128)}, s32[]{:T(128)}, /*index=5*/f32[2]{0:T(128)S(1)}, ...) while((s32[]{:T(128)}, f32[3,128,128]{2,1,0:T(8,128)S(1)}, ...), condition=%wide.region_5.10_spmd, body=%wide.region_4.9_spmd.sunk | while | flops 279037440 | bytes 5914997 | solution.py:17
  129.1 11.7 %custom-call.110 = f32[128,128]{1,0:T(8,128)S(1)} custom-call(f32[128,128]{1,0:T(8,128)S(1)} %fusion.617), custom_call_target="Cholesky" | custom-call | tf_op jit(solution)/shard_map/while/body/jit(cholesky)/cholesky/custom-call.1 | solution.py:87
  143.2 11.7 %custom-call.111 = f32[128,128]{1,0:T(8,128)S(1)} custom-call(f32[128,128]{1,0:T(8,128)S(1)} %fusion.620), custom_call_target="Cholesky" | custom-call | tf_op jit(solution)/shard_map/while/body/jit(cholesky)/cholesky/custom-call.1 | solution.py:90
  156.3 9.8 %custom-call.112 = f32[1,128,128]{1,2,0:T(8,128)S(1)} custom-call(f32[1,128,128]{2,1,0:T(8,128)S(1)} %fusion.621), custom_call_target="InvertDiagBlocksLowerTriangular" | custom-call | tf_op jit(solution)/shard_map/while/body/jit(_solve_triangular)/triangular_solve/custom-call.0 | solution.py:91
  173.5 11.7 %custom-call.68 = f32[128,128]{1,0:T(8,128)S(1)} custom-call(f32[128,128]{1,0:T(8,128)S(1)} %copy.255), custom_call_target="Cholesky" | custom-call | tf_op jit(solution)/shard_map/jit(cholesky)/cholesky/custom-call.1 | solution.py:87
  188.1 11.7 %custom-call.69 = f32[128,128]{1,0:T(8,128)S(1)} custom-call(f32[128,128]{1,0:T(8,128)S(1)} %copy.257), custom_call_target="Cholesky" | custom-call | tf_op jit(solution)/shard_map/jit(cholesky)/cholesky/custom-call.1 | solution.py:90
  201.2 9.8 %custom-call.70 = f32[1,128,128]{1,2,0:T(8,128)S(1)} custom-call(f32[1,128,128]{2,1,0:T(8,128)S(1)} %fusion.224), custom_call_target="InvertDiagBlocksLowerTriangular" | custom-call | tf_op jit(solution)/shard_map/jit(_solve_triangular)/triangular_solve/custom-call.0 | solution.py:91
  223.4 10.3 %all-reduce.2 = f32[4]{0:T(128)S(1)} all-reduce(f32[4]{0:T(128)S(1)} %dynamic-update-slice.2), channel_id=1, replica_groups=mesh['outer'=4,'inner'=2,'region'=4] {'outer'}, use_global_device_ids=true, to_apply=%add.2 | all-reduce | flops 4 | bytes 32
  249.3 134.8 %while.56 = (s32[]{:T(128)}, f32[3,128,128]{2,1,0:T(8,128)S(1)}, f32[2,128]{1,0:T(2,128)S(1)}, f32[]{:T(128)}, s32[]{:T(128)}, /*index=5*/f32[4]{0:T(128)S(1)}, ...) while((s32[]{:T(128)}, f32[3,128,128]{2,1,0:T(8,128)S(1)}, ...), condition=%wide.region_10.15_spmd, body=%wide.region_9.14_spmd.sunk | while | flops 279037440 | bytes 5914997 | solution.py:17
  250.1 11.7 %custom-call.113 = f32[128,128]{1,0:T(8,128)S(1)} custom-call(f32[128,128]{1,0:T(8,128)S(1)} %fusion.658), custom_call_target="Cholesky" | custom-call | tf_op jit(solution)/shard_map/while/body/jit(cholesky)/cholesky/custom-call.1 | solution.py:87
  264.5 11.7 %custom-call.114 = f32[128,128]{1,0:T(8,128)S(1)} custom-call(f32[128,128]{1,0:T(8,128)S(1)} %fusion.661), custom_call_target="Cholesky" | custom-call | tf_op jit(solution)/shard_map/while/body/jit(cholesky)/cholesky/custom-call.1 | solution.py:90
  277.5 9.8 %custom-call.115 = f32[1,128,128]{1,2,0:T(8,128)S(1)} custom-call(f32[1,128,128]{2,1,0:T(8,128)S(1)} %fusion.662), custom_call_target="InvertDiagBlocksLowerTriangular" | custom-call | tf_op jit(solution)/shard_map/while/body/jit(_solve_triangular)/triangular_solve/custom-call.0 | solution.py:91
  294.9 11.7 %custom-call.113 = f32[128,128]{1,0:T(8,128)S(1)} custom-call(f32[128,128]{1,0:T(8,128)S(1)} %fusion.658), custom_call_target="Cholesky" | custom-call | tf_op jit(solution)/shard_map/while/body/jit(cholesky)/cholesky/custom-call.1 | solution.py:87
  309.2 11.7 %custom-call.114 = f32[128,128]{1,0:T(8,128)S(1)} custom-call(f32[128,128]{1,0:T(8,128)S(1)} %fusion.661), custom_call_target="Cholesky" | custom-call | tf_op jit(solution)/shard_map/while/body/jit(cholesky)/cholesky/custom-call.1 | solution.py:90
  322.3 9.8 %custom-call.115 = f32[1,128,128]{1,2,0:T(8,128)S(1)} custom-call(f32[1,128,128]{2,1,0:T(8,128)S(1)} %fusion.662), custom_call_target="InvertDiagBlocksLowerTriangular" | custom-call | tf_op jit(solution)/shard_map/while/body/jit(_solve_triangular)/triangular_solve/custom-call.0 | solution.py:91
  339.6 11.7 %custom-call.113 = f32[128,128]{1,0:T(8,128)S(1)} custom-call(f32[128,128]{1,0:T(8,128)S(1)} %fusion.658), custom_call_target="Cholesky" | custom-call | tf_op jit(solution)/shard_map/while/body/jit(cholesky)/cholesky/custom-call.1 | solution.py:87
  354.0 11.7 %custom-call.114 = f32[128,128]{1,0:T(8,128)S(1)} custom-call(f32[128,128]{1,0:T(8,128)S(1)} %fusion.661), custom_call_target="Cholesky" | custom-call | tf_op jit(solution)/shard_map/while/body/jit(cholesky)/cholesky/custom-call.1 | solution.py:90
  367.0 9.8 %custom-call.115 = f32[1,128,128]{1,2,0:T(8,128)S(1)} custom-call(f32[1,128,128]{2,1,0:T(8,128)S(1)} %fusion.662), custom_call_target="InvertDiagBlocksLowerTriangular" | custom-call | tf_op jit(solution)/shard_map/while/body/jit(_solve_triangular)/triangular_solve/custom-call.0 | solution.py:91
  384.4 11.7 %custom-call.71 = f32[128,128]{1,0:T(8,128)S(1)} custom-call(f32[128,128]{1,0:T(8,128)S(1)} %fusion.244), custom_call_target="Cholesky" | custom-call | tf_op jit(solution)/shard_map/jit(cholesky)/cholesky/custom-call.1 | solution.py:87
  398.9 11.7 %custom-call.72 = f32[128,128]{1,0:T(8,128)S(1)} custom-call(f32[128,128]{1,0:T(8,128)S(1)} %copy.268), custom_call_target="Cholesky" | custom-call | tf_op jit(solution)/shard_map/jit(cholesky)/cholesky/custom-call.1 | solution.py:90
  412.0 9.8 %custom-call.73 = f32[1,128,128]{1,2,0:T(8,128)S(1)} custom-call(f32[1,128,128]{2,1,0:T(8,128)S(1)} %fusion.225), custom_call_target="InvertDiagBlocksLowerTriangular" | custom-call | tf_op jit(solution)/shard_map/jit(_solve_triangular)/triangular_solve/custom-call.0 | solution.py:91
  424.6 55.8 %while.57 = (s32[]{:T(128)}, f32[128]{0:T(128)S(1)}, f32[128,128]{1,0:T(8,128)S(1)}, f32[2,128]{1,0:T(2,128)S(1)}, f32[2,128,128]{2,1,0:T(8,128)S(1)}, /*index=5...) while((s32[]{:T(128)}, f32[128]{0:T(128)S(1)}, ...), condition=%wide.region_12.17_spmd, body=%wide.region_11.16_spmd.sunk | while | flops 126584960 | bytes 3097239 | solution.py:210
  427.4 11.7 %custom-call.119 = f32[128,128]{1,0:T(8,128)S(1)} custom-call(f32[128,128]{1,0:T(8,128)S(1)} %fusion.693), custom_call_target="Cholesky" | custom-call | tf_op jit(solution)/shard_map/while/body/eval_jaxpr/jit(cholesky)/cholesky/custom-call.1 | solution.py:37
  455.2 11.7 %custom-call.119 = f32[128,128]{1,0:T(8,128)S(1)} custom-call(f32[128,128]{1,0:T(8,128)S(1)} %fusion.693), custom_call_target="Cholesky" | custom-call | tf_op jit(solution)/shard_map/while/body/eval_jaxpr/jit(cholesky)/cholesky/custom-call.1 | solution.py:37
  (423 shorter events, 147.3 us)
Async XLA Ops:
  7.2 233.3 %all-reduce.6.cloned.1.call-start = ((), (), s32[]{:S(2)}) async-start(), calls=%async_computation | async-start | bytes 393216 | tf_op jit(solution)/shard_map/psum | solution.py:22
  7.2 0.7 copy-start.14
  7.9 0.7 copy-start.8
  8.6 1.5 copy-start.5
  10.1 0.8 copy-start.6
  10.1 0.8 copy-start.10
  10.1 0.8 copy-start.11
  10.8 0.7 copy-start.7
  10.8 0.7 copy-start.9
  71.1 2.0 copy-start
  71.1 0.7 copy-start.16
  123.9 4.3 copy-start.4
  173.1 42.4 %copy-start.2 = (f32[3,128,128]{2,1,0:T(8,128)}, f32[3,128,128]{2,1,0:T(8,128)S(1)}, u32[]{:S(2)}) copy-start(f32[3,128,128]{2,1,0:T(8,128)S(1)} %get-tuple-element.386) | copy-start | bytes 589828
  215.8 0.7 copy-start.15
  239.7 9.6 %copy-start.1 = (f32[3,128,128]{2,1,0:T(8,128)S(1)}, f32[3,128,128]{2,1,0:T(8,128)}, u32[]{:S(2)}) copy-start(f32[3,128,128]{2,1,0:T(8,128)} %copy-done) | copy-start | bytes 589828
  421.8 1.4 copy-start.3
  480.5 0.7 copy-start.12
  480.5 0.6 copy-start.13
Sparse Core Ops, SparseCore 0:
  215.0 25.4 all-reduce.5
where the time goes:
time: 496 us; the launch traced here: 488 us
  other arithmetic  341 us (69%)
  matrix products  46.1 us (9%)
  blocking collectives  42.1 us (8%)
  local copies, waits for them, and re-layouts  26.3 us (5%)
  loops' own time  16.3 us (3%)
  between operations  15.2 us (3%)
    another operation x21, other arithmetic, blend_parts(): core_root = jnp.linalg.cholesky(core)  87 us
    another operation x21, other arithmetic, blend_parts(): jnp.linalg.cholesky(early_spread + (1.0 - early_live) * ident_mat)  86.9 us
    another operation x14, other arithmetic, blend_parts(): jax.scipy.linalg.solve_triangular(core_root, spread_root.T, lower=True)  73.2 us
    dot_general x125, matrix products, highest(): return jnp.dot(left, right, precision=lax.Precision.HIGHEST)  36.9 us
    another operation x6, other arithmetic, filter_step(): factor = jnp.linalg.cholesky(innov_cov)  24.8 us
    another operation x6, other arithmetic, step_element(): factor = jnp.linalg.cholesky(innov_cov)  24.8 us
    all_gather x4, blocking collectives, entering(): gathered = jax.tree.map(lambda a: lax.all_gather(a, axis), part)  22.9 us
    another operation x4, other arithmetic, filter_step(): solved = jax.scipy.linalg.cho_solve((factor, True), picked)  20.9 us
  transfers between devices with their start and end apart: 1, of which 1 were waited for; matrix products, arithmetic and copies ran while one was open for 1% of the time, Pallas kernels for 0%

commit v1 on v0

v1 whole, which is shorter than its diff:
```python
import jax
import jax.numpy as jnp
from jax import lax
from jax.experimental import pallas as pl
from jax.experimental.pallas import tpu as pltpu
from jax.sharding import PartitionSpec as P

SERIES_BOUND = 1e-3
TIME_AXES = ("outer", "inner")


def split(value):
    high = value.astype(jnp.bfloat16)
    return high, (value - high.astype(jnp.float32)).astype(jnp.bfloat16)


def dot3(left, right):
    left_high, left_low = split(left)
    right_high, right_low = split(right)

    def product(a, b):
        return jnp.dot(a, b, preferred_element_type=jnp.float32)

    return product(left_high, right_high) + (
        product(left_high, right_low) + product(left_low, right_high)
    )


def dot_full(left, right):
    return lax.dot_general(
        left, right, (((1,), (0,)), ((), ())),
        precision=lax.Precision.HIGHEST, preferred_element_type=jnp.float32,
    )


def dot_full_nt(left, right):
    return lax.dot_general(
        left, right, (((1,), (1,)), ((), ())),
        precision=lax.Precision.HIGHEST, preferred_element_type=jnp.float32,
    )


def gather_steps(rows, parts):
    gathered = rows[None]
    reach = 1
    while reach < parts:
        pairs = [(i, i ^ reach) for i in range(parts)]
        gathered = jnp.concatenate([gathered, lax.ppermute(gathered, TIME_AXES, pairs)], 0)
        reach *= 2
    return gathered


def kernel(
    own_ref, steps_ref, map_ref, trans_ref, noise_ref, var_ref, mean_ref, prior_ref,
    mean_out, cov_out, prec_ref, info_ref, state_ref, check_ref, trans_t_ref,
):
    parts, rows_each, width = steps_ref.shape
    per_part = rows_each // 2
    size = trans_ref.shape[0]
    own = own_ref[0]
    first = own * per_part
    row_ids = lax.broadcasted_iota(jnp.int32, (size, size), 0)
    col_ids = lax.broadcasted_iota(jnp.int32, (size, size), 1)
    on_diag = row_ids == col_ids

    inv_var = 1.0 / var_ref[...]

    def place(source, carried):
        block = steps_ref[source ^ own]
        weight = block[per_part:] * inv_var
        prec_ref[pl.ds(source * per_part, per_part), :] = weight
        info_ref[pl.ds(source * per_part, per_part), :] = weight * block[:per_part]
        return carried

    lax.fori_loop(0, parts, place, 0, unroll=parts <= 8)
    chosen = (row_ids == map_ref[...]).astype(jnp.float32)
    prec_ref[...] = dot_full_nt(prec_ref[...], chosen)
    info_ref[...] = dot_full_nt(info_ref[...], chosen)

    trans = trans_ref[...]
    noise = noise_ref[...]
    trans_t = trans.T
    trans_t_ref[...] = trans_t
    pad = jnp.zeros((7, size), jnp.float32)
    check_ref[...] = jnp.zeros_like(check_ref)

    def start():
        cov = dot3(trans * prior_ref[...], trans_t_ref[...]) + noise
        mean = dot3(jnp.broadcast_to(mean_ref[...], (8, size)), trans_t_ref[...])
        return cov, mean

    def factors(cov, mean, step):
        prec = prec_ref[pl.ds(step, 1), :]
        info = info_ref[pl.ds(step, 1), :]
        own_var = jnp.sum(jnp.where(on_diag, cov, 0.0), axis=0, keepdims=True)
        shrink = 1.0 / (1.0 + own_var * prec)
        series = jnp.where(on_diag, 0.0, cov * (prec * shrink))
        push = (info - prec * mean) * shrink
        return shrink, series, push

    def advance(cov, mean, step, outs):
        shrink, series, push = factors(cov, mean, step)
        trans_t = trans_t_ref[...]
        left = [trans_ref[...] * shrink, push]
        if outs:
            left.append(jnp.where(on_diag, jnp.broadcast_to(shrink, (size, size)), 0.0))
        left = jnp.concatenate(left, 0)
        first_pow = dot3(jnp.concatenate([series, left], 0), series)
        pow2, left1 = first_pow[:size], first_pow[size:]
        moved = dot3(jnp.concatenate([cov, mean], 0), trans_t)
        right0, mean0 = moved[:size], moved[size:]
        second = dot3(jnp.concatenate([pow2, series, left1], 0), pow2)
        pow4, pow3, left3 = second[:size], second[size : 2 * size], second[2 * size :]
        check_ref[step] = jnp.sum((pow4 * pow4).reshape(size // 8, 8, size), axis=0)
        left = left - left3
        left = left + dot3(left, 2.0 * pow2 - series - pow3 + pow4)
        even = pow4 - pow2
        if outs:
            right0 = jnp.concatenate([right0, cov], 1)
        right = right0 + dot3(even, right0)
        final = dot3(left[: size + 8], right[:, :size])
        cov_next, mean_next = final[:size] + noise_ref[...], final[size:] + mean0
        if not outs:
            return cov_next, mean_next
        filt = dot3(left[size:], right[:, size:])
        return cov_next, mean_next, filt[8:], filt[:8] + mean

    cov, mean = start()

    def body(step, carried):
        return advance(*carried, step, False)

    cov, mean = lax.fori_loop(0, first, body, (cov, mean))
    for j in range(per_part):
        cov, mean, filt_cov, filt_mean = advance(cov, mean, first + j, True)
        cov_out[j] = 0.5 * (filt_cov + filt_cov.T)
        mean_out[pl.ds(j, 1), :] = filt_mean[:1]

    sizes = jnp.sum(jnp.sum(check_ref[...], axis=1), axis=1, keepdims=True)
    failed = jnp.sum(jnp.where(sizes <= SERIES_BOUND, 0.0, 1.0))

    @pl.when(failed > 0.0)
    def _():
        lane = lax.broadcasted_iota(jnp.int32, (1, size), 1)

        def absorb(step, mean):
            prec = prec_ref[pl.ds(step, 1), :]
            info = info_ref[pl.ds(step, 1), :]

            def one(s, mean):
                here = lane == s

                def at(row):
                    return jnp.sum(jnp.where(here, row, 0.0), axis=1, keepdims=True)

                cov = state_ref[...]
                row = state_ref[pl.ds(s, 1), :]
                col = jnp.sum(jnp.where(here, cov, 0.0), axis=1, keepdims=True)
                scale = 1.0 / (1.0 + at(prec) * at(row))
                state_ref[...] = cov - col * (row * (at(prec) * scale))
                return mean + row * ((at(info) - at(prec) * at(mean)) * scale)

            mean = lax.fori_loop(0, size, one, mean)
            cov = state_ref[...]
            state_ref[...] = 0.5 * (cov + cov.T)
            return mean

        def predict(mean):
            cov = dot_full(dot_full(trans_ref[...], state_ref[...]), trans_t_ref[...])
            state_ref[...] = cov + noise_ref[...]
            return dot_full(jnp.broadcast_to(mean, (8, size)), trans_t_ref[...])[:1]

        state_ref[...] = dot_full(trans_ref[...] * prior_ref[...], trans_t_ref[...]) + noise_ref[...]
        mean = dot_full(jnp.broadcast_to(mean_ref[...], (8, size)), trans_t_ref[...])[:1]
        mean = lax.fori_loop(0, first, lambda t, m: predict(absorb(t, m)), mean)
        for j in range(per_part):
            mean = absorb(first + j, mean)
            cov_out[j] = state_ref[...]
            mean_out[pl.ds(j, 1), :] = mean
            if j + 1 < per_part:
                mean = predict(mean)


def local(
    observations, obs_mask, sensor_map, transition, proc_noise, obs_var, prior_mean, prior_var
):
    steps_here, sensors = observations.shape
    size = transition.shape[0]
    parts = lax.axis_size("outer") * lax.axis_size("inner")
    position = lax.axis_index("outer") * lax.axis_size("inner") + lax.axis_index("inner")
    rows = jnp.concatenate([observations, obs_mask.astype(jnp.float32)], 0)
    gathered = gather_steps(rows, parts)
    steps = parts * steps_here
    vmem = pl.BlockSpec(memory_space=pltpu.VMEM)
    return pl.pallas_call(
        kernel,
        out_shape=(
            jax.ShapeDtypeStruct((steps_here, size), jnp.float32),
            jax.ShapeDtypeStruct((steps_here, size, size), jnp.float32),
        ),
        in_specs=[pl.BlockSpec(memory_space=pltpu.SMEM)] + [vmem] * 7,
        out_specs=(vmem, vmem),
        scratch_shapes=[
            pltpu.VMEM((steps, sensors), jnp.float32),
            pltpu.VMEM((steps, sensors), jnp.float32),
            pltpu.VMEM((size, size), jnp.float32),
            pltpu.VMEM((steps, 8, size), jnp.float32),
            pltpu.VMEM((size, size), jnp.float32),
        ],
        name="filter_window",
    )(
        position.astype(jnp.int32)[None], gathered, sensor_map[None], transition, proc_noise,
        obs_var[None], prior_mean[None], prior_var[None],
    )


def solution(mesh):
    return jax.shard_map(
        local,
        mesh=mesh,
        in_specs=(
            P(("region", "outer", "inner"), None),
            P(("region", "outer", "inner"), None),
            P("region"),
            P(),
            P(),
            P(),
            P("region"),
            P("region"),
        ),
        out_specs=(
            P(("region", "outer", "inner"), None),
            P(("region", "outer", "inner"), None, None),
        ),
        check_vma=False,
    )
```

time: 496 us -> 31.8 us (0.06); the launches traced: 488 us -> 31.6 us
  other arithmetic: 341 us -> 1.31 us
  matrix products: 46.1 us -> 0 us
  blocking collectives: 42.1 us -> 0 us
  local copies, waits for them, and re-layouts: 26.3 us -> 0.01 us
  Pallas kernels: 0 us -> 22 us
  loops' own time: 16.3 us -> 0 us
  between operations: 15.2 us -> 0.64 us
    another operation x88 -> x0, other arithmetic: 339 us -> none  [the longest x21 87 us: blend_parts(): core_root = jnp.linalg.cholesky(core)]
    dot_general x125 -> x0, matrix products: 36.9 us -> none  [highest(): return jnp.dot(left, right, precision=lax.Precision.HIGHEST)]
    all_gather x4 -> x0, blocking collectives: 22.9 us -> none  [entering(): gathered = jax.tree.map(lambda a: lax.all_gather(a, axis), part)]
    pallas_call x0 -> x1, Pallas kernels: none -> 22 us  [local(): pl.pallas_call(kernel, out_shape=(jax.ShapeDtypeStruct((steps_here, size)...]
    another operation x4 -> x0, loops' own time: 16.3 us -> none  [the longest x2 9.47 us: entering(): return lax.fori_loop(0, place, one, state)]
    unnamed x2 -> x0, blocking collectives: 14.3 us -> none
    gather x19 -> x0, local copies, waits for them, and re-layouts: 10.4 us -> none  [the longest x2 2.45 us: filter_step(): innovation = weights * (observed - pred_mean[sensor_map])]
    another operation x19 -> x0, matrix products: 9.19 us -> none  [the longest x7 6.29 us: blend_parts(): jax.scipy.linalg.solve_triangular(core_root, spread_root.T, lower=True)]
  transfers between devices with their start and end apart: 1 -> 3, of which waited for: 1 -> 3; matrix products, arithmetic and copies ran while one was open for 1% -> 0% of each run, Pallas kernels for 0% -> 0%
where the time goes in v1:
time: 31.8 us; the launch traced here: 31.6 us
  Pallas kernels  22 us (69%)
  waiting for transfers between devices  5.28 us (17%)
  starting transfers between devices  2.37 us (7%)
  other arithmetic  1.31 us (4%)
  between operations  0.64 us (2%)
    pallas_call x1, Pallas kernels, local(): pl.pallas_call(kernel, out_shape=(jax.ShapeDtypeStruct((steps_here, size)...  22 us
    ppermute x3, waiting for transfers between devices, gather_steps(): lax.ppermute(gathered, TIME_AXES, pairs)  5.28 us
    ppermute x3, starting transfers between devices, gather_steps(): lax.ppermute(gathered, TIME_AXES, pairs)  2.37 us
    convert_element_type x1, other arithmetic, local(): rows = jnp.concatenate([observations, obs_mask.astype(jnp.float32)], 0)  0.69 us
  transfers between devices with their start and end apart: 3, of which 3 were waited for; matrix products, arithmetic and copies ran while one was open for 0% of the time, Pallas kernels for 0%

profile of v1, /device:TPU:31, one launch (start us, length us, event | category | flops | bytes accessed | tf_op | source)
XLA Modules:
  0.0 31.6 jit_solution(10765972426486454220)
XLA Ops:
  0.6 0.0 copy-start
  0.6 0.7 %convert_element_type.3 = f32[2,128]{1,0:T(2,128)S(1)} convert(s32[2,128]{1,0:T(2,128)} %param.9) | non-fusion elementwise | flops 256 | bytes 2048 | tf_op jit(solution)/shard_map/convert_element_type | solution.py:191
  1.3 0.0 copy-done
  1.3 0.3 %collective-permute-start = (f32[1,4,128]{2,1,0:T(4,128)S(1)}, f32[1,4,128]{2,1,0:T(4,128)S(1)}, u32[]{:S(2)}, u32[]{:S(2)}) collective-permute-start(f32[1,4,128]{2,1,0:T(4,128)S(1)} %maximum_bitcast_fusion), channel_id=1, source_target_pairs={{0,4},{4,0},{8,12},{12,8},{16,20},{20,16},{24,28},{28,24},{1,5},{5... | collective-permute-start | bytes 6152 | tf_op jit(solution)/shard_map/ppermute | solution.py:48
  1.7 2.2 %collective-permute-done = f32[1,4,128]{2,1,0:T(4,128)S(1)} collective-permute-done((f32[1,4,128]{2,1,0:T(4,128)S(1)}, f32[1,4,128]{2,1,0:T(4,128)S(1)}, u32[]{:S(2)}, u32[]{:S(2)}) %collective-permute-start) | collective-permute-done | bytes 2080 | tf_op jit(solution)/shard_map/ppermute | solution.py:48
  3.8 1.8 %collective-permute-start.1 = (f32[2,4,128]{2,1,0:T(4,128)S(1)}, f32[2,4,128]{2,1,0:T(4,128)S(1)}, u32[]{:S(2)}, u32[]{:S(2)}) collective-permute-start(f32[2,4,128]{2,1,0:T(4,128)S(1)} %pad_maximum_fusion.2), channel_id=1, source_target_pairs={{0,8},{4,12},{8,0},{12,4},{16,24},{20,28},{24,16},{28,20},{1,9},{5... | collective-permute-start | bytes 12296 | tf_op jit(solution)/shard_map/ppermute | solution.py:48
  5.7 0.8 %collective-permute-done.1 = f32[2,4,128]{2,1,0:T(4,128)S(1)} collective-permute-done((f32[2,4,128]{2,1,0:T(4,128)S(1)}, f32[2,4,128]{2,1,0:T(4,128)S(1)}, u32[]{:S(2)}, u32[]{:S(2)}) %collective-permute-start.1) | collective-permute-done | bytes 4128 | tf_op jit(solution)/shard_map/ppermute | solution.py:48
  6.5 0.2 collective-permute-start.2
  6.7 2.3 %collective-permute-done.2 = f32[4,4,128]{2,1,0:T(4,128)S(1)} collective-permute-done((f32[4,4,128]{2,1,0:T(4,128)S(1)}, f32[4,4,128]{2,1,0:T(4,128)S(1)}, u32[]{:S(2)}, u32[]{:S(2)}) %collective-permute-start.2) | collective-permute-done | bytes 8224 | tf_op jit(solution)/shard_map/ppermute | solution.py:48
  9.0 0.6 %pad_maximum_fusion.steps_ref = f32[8,4,128]{2,1,0:T(4,128)} fusion(f32[4,4,128]{2,1,0:T(4,128)S(1)} %collective-permute-done.2, f32[2,4,128]{2,1,0:T(4,128)S(1)} %collective-permute-done.1, f32[1,4,128]{2,1,0:T(4,128)S(1)} %collective-permute-done, f32[1,4,128]{2,1,0:T(4,128)S(1)} %maximum_bitcast_fusion), kind=kLoop, calls=%fused_computation | loop fusion | flops 12288 | bytes 32768 | tf_op jit(solution)/shard_map/concatenate | solution.py:48
  9.6 22.0 %filter_window.1 = (f32[2,128]{1,0:T(2,128)}, f32[2,128,128]{2,1,0:T(8,128)}) custom-call(s32[1]{0:T(128)} %bitcast.own_ref, f32[8,4,128]{2,1,0:T(4,128)} %pad_maximum_fusion.steps_ref, s32[1,128]{1,0:T(1,128)} %bitcast.7, f32[128,128]{1,0:T(8,128)} %trans_ref.1, f32[128,128]{1,0:T(8,128)} %noise_ref.1, f32[1,128]{1,0:T(1,128)} %bitcast.8, ...), custom_call_target="tpu_custom_call" | custom-call | tf_op jit(solution)/shard_map/filter_window/pallas_call | solution.py:195
  (3 shorter events, 0.0 us)
Async XLA Ops:
  0.6 0.7 %copy-start = (f32[2,128]{1,0:T(2,128)S(1)}, f32[2,128]{1,0:T(2,128)}, u32[]{:S(2)}) copy-start(f32[2,128]{1,0:T(2,128)} %param.8) | copy-start | bytes 3076
  1.3 2.5 %collective-permute-start = (f32[1,4,128]{2,1,0:T(4,128)S(1)}, f32[1,4,128]{2,1,0:T(4,128)S(1)}, u32[]{:S(2)}, u32[]{:S(2)}) collective-permute-start(f32[1,4,128]{2,1,0:T(4,128)S(1)} %maximum_bitcast_fusion), channel_id=1, source_target_pairs={{0,4},{4,0},{8,12},{12,8},{16,20},{20,16},{24,28},{28,24},{1,5},{5... | collective-permute-start | bytes 6152 | tf_op jit(solution)/shard_map/ppermute | solution.py:48
  3.8 2.6 %collective-permute-start.1 = (f32[2,4,128]{2,1,0:T(4,128)S(1)}, f32[2,4,128]{2,1,0:T(4,128)S(1)}, u32[]{:S(2)}, u32[]{:S(2)}) collective-permute-start(f32[2,4,128]{2,1,0:T(4,128)S(1)} %pad_maximum_fusion.2), channel_id=1, source_target_pairs={{0,8},{4,12},{8,0},{12,4},{16,24},{20,28},{24,16},{28,20},{1,9},{5... | collective-permute-start | bytes 12296 | tf_op jit(solution)/shard_map/ppermute | solution.py:48
  6.5 2.5 %collective-permute-start.2 = (f32[4,4,128]{2,1,0:T(4,128)S(1)}, f32[4,4,128]{2,1,0:T(4,128)S(1)}, u32[]{:S(2)}, u32[]{:S(2)}) collective-permute-start(f32[4,4,128]{2,1,0:T(4,128)S(1)} %pad_maximum_fusion.1), channel_id=1, source_target_pairs={{0,16},{4,20},{8,24},{12,28},{16,0},{20,4},{24,8},{28,12},{1,17},{... | collective-permute-start | bytes 24584 | tf_op jit(solution)/shard_map/ppermute | solution.py:48

commit v2 on v1

--- a/solution.py
+++ b/solution.py
@@ -1,3 +1,5 @@
+import math
+
 import jax
 import jax.numpy as jnp
 from jax import lax
@@ -5,8 +7,20 @@
 from jax.experimental.pallas import tpu as pltpu
 from jax.sharding import PartitionSpec as P
 
-SERIES_BOUND = 1e-3
+RADIUS = 0.6
+SERIES_BOUND = RADIUS**8
 TIME_AXES = ("outer", "inner")
+
+
+def series_factors():
+    squeeze = 1.0 - RADIUS**2
+
+    def quartic(k):
+        cosine = math.cos(k * math.pi / 6)
+        const = cosine**2 + squeeze * math.sin(k * math.pi / 6) ** 2
+        return 2.0 * const - 4.0 * cosine**2, const**2
+
+    return squeeze, quartic(2), quartic(1)
 
 
 def split(value):
@@ -14,16 +28,19 @@
     return high, (value - high.astype(jnp.float32)).astype(jnp.bfloat16)
 
 
+def mul(left, right):
+    size = right[0].shape[1]
+    columns = jnp.concatenate(right, 1)
+    result = jnp.dot(
+        jnp.concatenate(left, 1),
+        jnp.concatenate([columns, columns], 0),
+        preferred_element_type=jnp.float32,
+    )
+    return result[:, :size] + result[:, size:]
+
+
 def dot3(left, right):
-    left_high, left_low = split(left)
-    right_high, right_low = split(right)
-
-    def product(a, b):
-        return jnp.dot(a, b, preferred_element_type=jnp.float32)
-
-    return product(left_high, right_high) + (
-        product(left_high, right_low) + product(left_low, right_high)
-    )
+    return mul(split(left), split(right))
 
 
 def dot_full(left, right):
@@ -98,41 +115,56 @@
         push = (info - prec * mean) * shrink
         return shrink, series, push
 
-    def advance(cov, mean, step, outs):
+    square, wide, narrow = series_factors()
+
+    def advance(cov, mean, step, move, outs):
         shrink, series, push = factors(cov, mean, step)
-        trans_t = trans_t_ref[...]
-        left = [trans_ref[...] * shrink, push]
+        series = split(series)
+        pow2 = mul(series, series)
+        lefts = []
+        rights = []
+        if move:
+            lefts.append(trans_ref[...] * shrink)
+            moved = mul(split(jnp.concatenate([cov, mean], 0)), split(trans_t_ref[...]))
+            rights.append(moved[:size])
         if outs:
-            left.append(jnp.where(on_diag, jnp.broadcast_to(shrink, (size, size)), 0.0))
-        left = jnp.concatenate(left, 0)
-        first_pow = dot3(jnp.concatenate([series, left], 0), series)
-        pow2, left1 = first_pow[:size], first_pow[size:]
-        moved = dot3(jnp.concatenate([cov, mean], 0), trans_t)
-        right0, mean0 = moved[:size], moved[size:]
-        second = dot3(jnp.concatenate([pow2, series, left1], 0), pow2)
-        pow4, pow3, left3 = second[:size], second[size : 2 * size], second[2 * size :]
+            lefts.append(jnp.where(on_diag, jnp.broadcast_to(shrink, (size, size)), 0.0))
+            rights.append(cov)
+        lefts[-1] = jnp.concatenate([lefts[-1], push], 0)
+        pow2_split = split(pow2)
+        pow4 = jnp.dot(pow2_split[0], pow2_split[0], preferred_element_type=jnp.float32)
         check_ref[step] = jnp.sum((pow4 * pow4).reshape(size // 8, 8, size), axis=0)
-        left = left - left3
-        left = left + dot3(left, 2.0 * pow2 - series - pow3 + pow4)
-        even = pow4 - pow2
+        even_left = split(pow4 * (1.0 / wide[1]) + pow2 * (wide[0] / wide[1]))
+        even_right = split(pow4 * (1.0 / narrow[1]) + pow2 * (narrow[0] / narrow[1]))
+        pow2_scaled = split(pow2 * (1.0 / square))
+        done = []
+        for left in lefts:
+            left = left - mul(split(left), series)
+            left = left + mul(split(left), pow2_scaled)
+            done.append(split(left + mul(split(left), even_left)))
+        rights = [split(right + mul(even_right, split(right))) for right in rights]
+        result = []
+        if move:
+            final = mul(done[0], rights[0])
+            mean_next = final[size:] if not outs else mul(tuple(x[size:] for x in done[1]), rights[0])
+            result += [final[:size] + noise_ref[...], mean_next + moved[size:]]
         if outs:
-            right0 = jnp.concatenate([right0, cov], 1)
-        right = right0 + dot3(even, right0)
-        final = dot3(left[: size + 8], right[:, :size])
-        cov_next, mean_next = final[:size] + noise_ref[...], final[size:] + mean0
-        if not outs:
-            return cov_next, mean_next
-        filt = dot3(left[size:], right[:, size:])
-        return cov_next, mean_next, filt[8:], filt[:8] + mean
+            final = mul(done[-1], rights[-1])
+            result += [final[:size], final[size:] + mean]
+        return result
 
     cov, mean = start()
 
     def body(step, carried):
-        return advance(*carried, step, False)
+        return tuple(advance(*carried, step, True, False))
 
     cov, mean = lax.fori_loop(0, first, body, (cov, mean))
     for j in range(per_part):
-        cov, mean, filt_cov, filt_mean = advance(cov, mean, first + j, True)
+        moves = j + 1 < per_part
+        result = advance(cov, mean, first + j, moves, True)
+        if moves:
+            cov, mean = result[:2]
+        filt_cov, filt_mean = result[-2:]
         cov_out[j] = 0.5 * (filt_cov + filt_cov.T)
         mean_out[pl.ds(j, 1), :] = filt_mean[:1]
 

time: 31.8 us -> 23 us (0.72)
  Pallas kernels: 22 us -> 13.2 us
    pallas_call x1, Pallas kernels: 22 us -> 13.2 us  [local(): pl.pallas_call(kernel, out_shape=(jax.ShapeDtypeStruct((steps_here, size)...]
where the time goes in v2:
time: 23 us; the launch traced here: 22.8 us
  Pallas kernels  13.2 us (57%)
  waiting for transfers between devices  5.28 us (23%)
  starting transfers between devices  2.37 us (10%)
  other arithmetic  1.31 us (6%)
  between operations  0.64 us (3%)
    pallas_call x1, Pallas kernels, local(): pl.pallas_call(kernel, out_shape=(jax.ShapeDtypeStruct((steps_here, size)...  13.2 us
    ppermute x3, waiting for transfers between devices, gather_steps(): lax.ppermute(gathered, TIME_AXES, pairs)  5.28 us
    ppermute x3, starting transfers between devices, gather_steps(): lax.ppermute(gathered, TIME_AXES, pairs)  2.37 us
    convert_element_type x1, other arithmetic, local(): rows = jnp.concatenate([observations, obs_mask.astype(jnp.float32)], 0)  0.69 us
    concatenate x3, other arithmetic, gather_steps(): jnp.concatenate([gathered, lax.ppermute(gathered, TIME_AXES, pairs)], 0)  0.61 us
  transfers between devices with their start and end apart: 3, of which 3 were waited for; matrix products, arithmetic and copies ran while one was open for 0% of the time, Pallas kernels for 0%

profile of v2, /device:TPU:31, one launch (start us, length us, event | category | flops | bytes accessed | tf_op | source)
XLA Modules:
  0.0 22.8 jit_solution(7726175218903404895)
XLA Ops:
  0.6 0.0 copy-start
  0.6 0.7 %convert_element_type.3 = f32[2,128]{1,0:T(2,128)S(1)} convert(s32[2,128]{1,0:T(2,128)} %param.9) | non-fusion elementwise | flops 256 | bytes 2048 | tf_op jit(solution)/shard_map/convert_element_type | solution.py:223
  1.3 0.0 copy-done
  1.3 0.3 %collective-permute-start = (f32[1,4,128]{2,1,0:T(4,128)S(1)}, f32[1,4,128]{2,1,0:T(4,128)S(1)}, u32[]{:S(2)}, u32[]{:S(2)}) collective-permute-start(f32[1,4,128]{2,1,0:T(4,128)S(1)} %maximum_bitcast_fusion), channel_id=1, source_target_pairs={{0,4},{4,0},{8,12},{12,8},{16,20},{20,16},{24,28},{28,24},{1,5},{5... | collective-permute-start | bytes 6152 | tf_op jit(solution)/shard_map/ppermute | solution.py:65
  1.7 2.2 %collective-permute-done = f32[1,4,128]{2,1,0:T(4,128)S(1)} collective-permute-done((f32[1,4,128]{2,1,0:T(4,128)S(1)}, f32[1,4,128]{2,1,0:T(4,128)S(1)}, u32[]{:S(2)}, u32[]{:S(2)}) %collective-permute-start) | collective-permute-done | bytes 2080 | tf_op jit(solution)/shard_map/ppermute | solution.py:65
  3.8 1.8 %collective-permute-start.1 = (f32[2,4,128]{2,1,0:T(4,128)S(1)}, f32[2,4,128]{2,1,0:T(4,128)S(1)}, u32[]{:S(2)}, u32[]{:S(2)}) collective-permute-start(f32[2,4,128]{2,1,0:T(4,128)S(1)} %pad_maximum_fusion.2), channel_id=1, source_target_pairs={{0,8},{4,12},{8,0},{12,4},{16,24},{20,28},{24,16},{28,20},{1,9},{5... | collective-permute-start | bytes 12296 | tf_op jit(solution)/shard_map/ppermute | solution.py:65
  5.7 0.8 %collective-permute-done.1 = f32[2,4,128]{2,1,0:T(4,128)S(1)} collective-permute-done((f32[2,4,128]{2,1,0:T(4,128)S(1)}, f32[2,4,128]{2,1,0:T(4,128)S(1)}, u32[]{:S(2)}, u32[]{:S(2)}) %collective-permute-start.1) | collective-permute-done | bytes 4128 | tf_op jit(solution)/shard_map/ppermute | solution.py:65
  6.5 0.2 collective-permute-start.2
  6.7 2.3 %collective-permute-done.2 = f32[4,4,128]{2,1,0:T(4,128)S(1)} collective-permute-done((f32[4,4,128]{2,1,0:T(4,128)S(1)}, f32[4,4,128]{2,1,0:T(4,128)S(1)}, u32[]{:S(2)}, u32[]{:S(2)}) %collective-permute-start.2) | collective-permute-done | bytes 8224 | tf_op jit(solution)/shard_map/ppermute | solution.py:65
  9.0 0.6 %pad_maximum_fusion.steps_ref = f32[8,4,128]{2,1,0:T(4,128)} fusion(f32[4,4,128]{2,1,0:T(4,128)S(1)} %collective-permute-done.2, f32[2,4,128]{2,1,0:T(4,128)S(1)} %collective-permute-done.1, f32[1,4,128]{2,1,0:T(4,128)S(1)} %collective-permute-done, f32[1,4,128]{2,1,0:T(4,128)S(1)} %maximum_bitcast_fusion), kind=kLoop, calls=%fused_computation | loop fusion | flops 12288 | bytes 32768 | tf_op jit(solution)/shard_map/concatenate | solution.py:65
  9.6 13.2 %filter_window.1 = (f32[2,128]{1,0:T(2,128)}, f32[2,128,128]{2,1,0:T(8,128)}) custom-call(s32[1]{0:T(128)} %bitcast.own_ref, f32[8,4,128]{2,1,0:T(4,128)} %pad_maximum_fusion.steps_ref, s32[1,128]{1,0:T(1,128)} %bitcast.7, f32[128,128]{1,0:T(8,128)} %trans_ref.1, f32[128,128]{1,0:T(8,128)} %noise_ref.1, f32[1,128]{1,0:T(1,128)} %bitcast.8, ...), custom_call_target="tpu_custom_call" | custom-call | tf_op jit(solution)/shard_map/filter_window/pallas_call | solution.py:227
  (3 shorter events, 0.0 us)
Async XLA Ops:
  0.6 0.7 %copy-start = (f32[2,128]{1,0:T(2,128)S(1)}, f32[2,128]{1,0:T(2,128)}, u32[]{:S(2)}) copy-start(f32[2,128]{1,0:T(2,128)} %param.8) | copy-start | bytes 3076
  1.3 2.5 %collective-permute-start = (f32[1,4,128]{2,1,0:T(4,128)S(1)}, f32[1,4,128]{2,1,0:T(4,128)S(1)}, u32[]{:S(2)}, u32[]{:S(2)}) collective-permute-start(f32[1,4,128]{2,1,0:T(4,128)S(1)} %maximum_bitcast_fusion), channel_id=1, source_target_pairs={{0,4},{4,0},{8,12},{12,8},{16,20},{20,16},{24,28},{28,24},{1,5},{5... | collective-permute-start | bytes 6152 | tf_op jit(solution)/shard_map/ppermute | solution.py:65
  3.8 2.6 %collective-permute-start.1 = (f32[2,4,128]{2,1,0:T(4,128)S(1)}, f32[2,4,128]{2,1,0:T(4,128)S(1)}, u32[]{:S(2)}, u32[]{:S(2)}) collective-permute-start(f32[2,4,128]{2,1,0:T(4,128)S(1)} %pad_maximum_fusion.2), channel_id=1, source_target_pairs={{0,8},{4,12},{8,0},{12,4},{16,24},{20,28},{24,16},{28,20},{1,9},{5... | collective-permute-start | bytes 12296 | tf_op jit(solution)/shard_map/ppermute | solution.py:65
  6.5 2.5 %collective-permute-start.2 = (f32[4,4,128]{2,1,0:T(4,128)S(1)}, f32[4,4,128]{2,1,0:T(4,128)S(1)}, u32[]{:S(2)}, u32[]{:S(2)}) collective-permute-start(f32[4,4,128]{2,1,0:T(4,128)S(1)} %pad_maximum_fusion.1), channel_id=1, source_target_pairs={{0,16},{4,20},{8,24},{12,28},{16,0},{20,4},{24,8},{28,12},{1,17},{... | collective-permute-start | bytes 24584 | tf_op jit(solution)/shard_map/ppermute | solution.py:65

commit v3 on v2

--- a/solution.py
+++ b/solution.py
@@ -46,13 +46,6 @@
 def dot_full(left, right):
     return lax.dot_general(
         left, right, (((1,), (0,)), ((), ())),
-        precision=lax.Precision.HIGHEST, preferred_element_type=jnp.float32,
-    )
-
-
-def dot_full_nt(left, right):
-    return lax.dot_general(
-        left, right, (((1,), (1,)), ((), ())),
         precision=lax.Precision.HIGHEST, preferred_element_type=jnp.float32,
     )
 
@@ -67,12 +60,35 @@
     return gathered
 
 
+def prepare(
+    map_ref, var_ref, trans_ref, noise_ref, mean_ref, prior_ref,
+    start_ref, turned_ref, chosen_ref, inv_var_ref,
+):
+    size = trans_ref.shape[0]
+    sensors = map_ref.shape[1]
+    trans = trans_ref[...]
+    turned = trans.T
+    turned_ref[...] = turned
+    rows = jnp.concatenate(
+        [trans * prior_ref[...], jnp.broadcast_to(mean_ref[...], (8, size))], 0
+    )
+    rows = dot3(rows, turned)
+    start_ref[:size] = rows[:size] + noise_ref[...]
+    start_ref[size:] = rows[size:]
+    components = lax.broadcasted_iota(jnp.int32, (size, sensors), 0)
+    chosen = (components == map_ref[...]).astype(jnp.float32)
+    chosen_ref[...] = chosen.T
+    inv_var_ref[...] = 1.0 / var_ref[...]
+
+
 def kernel(
-    own_ref, steps_ref, map_ref, trans_ref, noise_ref, var_ref, mean_ref, prior_ref,
-    mean_out, cov_out, prec_ref, info_ref, state_ref, check_ref, trans_t_ref,
+    own_ref, steps_ref, start_ref, turned_ref, chosen_ref, inv_var_ref, trans_ref, noise_ref,
+    mean_ref, prior_ref, mean_out, cov_out, prec_ref, info_ref, state_ref, check_ref, high_ref,
+    low_ref,
 ):
     parts, rows_each, width = steps_ref.shape
     per_part = rows_each // 2
+    steps = parts * per_part
     size = trans_ref.shape[0]
     own = own_ref[0]
     first = own * per_part
@@ -80,7 +96,7 @@
     col_ids = lax.broadcasted_iota(jnp.int32, (size, size), 1)
     on_diag = row_ids == col_ids
 
-    inv_var = 1.0 / var_ref[...]
+    inv_var = inv_var_ref[...]
 
     def place(source, carried):
         block = steps_ref[source ^ own]
@@ -90,21 +106,17 @@
         return carried
 
     lax.fori_loop(0, parts, place, 0, unroll=parts <= 8)
-    chosen = (row_ids == map_ref[...]).astype(jnp.float32)
-    prec_ref[...] = dot_full_nt(prec_ref[...], chosen)
-    info_ref[...] = dot_full_nt(info_ref[...], chosen)
-
-    trans = trans_ref[...]
-    noise = noise_ref[...]
-    trans_t = trans.T
-    trans_t_ref[...] = trans_t
-    pad = jnp.zeros((7, size), jnp.float32)
+    chosen = chosen_ref[...].astype(jnp.bfloat16)
+    left = jnp.concatenate([prec_ref[...], info_ref[...]], 0)
+    summed = jnp.zeros(left.shape, jnp.float32)
+    for _ in range(3):
+        part = left.astype(jnp.bfloat16)
+        left = left - part.astype(jnp.float32)
+        summed = summed + jnp.dot(part, chosen, preferred_element_type=jnp.float32)
+    prec_ref[...] = summed[:steps]
+    info_ref[...] = summed[steps:]
+    high_ref[...], low_ref[...] = split(turned_ref[...])
     check_ref[...] = jnp.zeros_like(check_ref)
-
-    def start():
-        cov = dot3(trans * prior_ref[...], trans_t_ref[...]) + noise
-        mean = dot3(jnp.broadcast_to(mean_ref[...], (8, size)), trans_t_ref[...])
-        return cov, mean
 
     def factors(cov, mean, step):
         prec = prec_ref[pl.ds(step, 1), :]
@@ -116,6 +128,7 @@
         return shrink, series, push
 
     square, wide, narrow = series_factors()
+    whole = 1.0 / (square * wide[1] * narrow[1])
 
     def advance(cov, mean, step, move, outs):
         shrink, series, push = factors(cov, mean, step)
@@ -124,25 +137,24 @@
         lefts = []
         rights = []
         if move:
-            lefts.append(trans_ref[...] * shrink)
-            moved = mul(split(jnp.concatenate([cov, mean], 0)), split(trans_t_ref[...]))
+            lefts.append(trans_ref[...] * (shrink * whole))
+            moved = mul(split(jnp.concatenate([cov, mean], 0)), (high_ref[...], low_ref[...]))
             rights.append(moved[:size])
         if outs:
-            lefts.append(jnp.where(on_diag, jnp.broadcast_to(shrink, (size, size)), 0.0))
+            lefts.append(jnp.where(on_diag, jnp.broadcast_to(shrink * whole, (size, size)), 0.0))
             rights.append(cov)
-        lefts[-1] = jnp.concatenate([lefts[-1], push], 0)
+        lefts[-1] = jnp.concatenate([lefts[-1], push * whole], 0)
         pow2_split = split(pow2)
         pow4 = jnp.dot(pow2_split[0], pow2_split[0], preferred_element_type=jnp.float32)
         check_ref[step] = jnp.sum((pow4 * pow4).reshape(size // 8, 8, size), axis=0)
-        even_left = split(pow4 * (1.0 / wide[1]) + pow2 * (wide[0] / wide[1]))
-        even_right = split(pow4 * (1.0 / narrow[1]) + pow2 * (narrow[0] / narrow[1]))
-        pow2_scaled = split(pow2 * (1.0 / square))
+        even_left = split(pow4 + pow2 * wide[0])
+        even_right = split(pow4 + pow2 * narrow[0])
         done = []
         for left in lefts:
             left = left - mul(split(left), series)
-            left = left + mul(split(left), pow2_scaled)
-            done.append(split(left + mul(split(left), even_left)))
-        rights = [split(right + mul(even_right, split(right))) for right in rights]
+            left = left * square + mul(split(left), pow2_split)
+            done.append(split(left * wide[1] + mul(split(left), even_left)))
+        rights = [split(right * narrow[1] + mul(even_right, split(right))) for right in rights]
         result = []
         if move:
             final = mul(done[0], rights[0])
@@ -153,7 +165,7 @@
             result += [final[:size], final[size:] + mean]
         return result
 
-    cov, mean = start()
+    cov, mean = start_ref[:size], start_ref[size:]
 
     def body(step, carried):
         return tuple(advance(*carried, step, True, False))
@@ -198,12 +210,12 @@
             return mean
 
         def predict(mean):
-            cov = dot_full(dot_full(trans_ref[...], state_ref[...]), trans_t_ref[...])
+            cov = dot_full(dot_full(trans_ref[...], state_ref[...]), turned_ref[...])
             state_ref[...] = cov + noise_ref[...]
-            return dot_full(jnp.broadcast_to(mean, (8, size)), trans_t_ref[...])[:1]
-
-        state_ref[...] = dot_full(trans_ref[...] * prior_ref[...], trans_t_ref[...]) + noise_ref[...]
-        mean = dot_full(jnp.broadcast_to(mean_ref[...], (8, size)), trans_t_ref[...])[:1]
+            return dot_full(jnp.broadcast_to(mean, (8, size)), turned_ref[...])[:1]
+
+        state_ref[...] = dot_full(trans_ref[...] * prior_ref[...], turned_ref[...]) + noise_ref[...]
+        mean = dot_full(jnp.broadcast_to(mean_ref[...], (8, size)), turned_ref[...])[:1]
         mean = lax.fori_loop(0, first, lambda t, m: predict(absorb(t, m)), mean)
         for j in range(per_part):
             mean = absorb(first + j, mean)
@@ -224,25 +236,45 @@
     gathered = gather_steps(rows, parts)
     steps = parts * steps_here
     vmem = pl.BlockSpec(memory_space=pltpu.VMEM)
+
+    def near(*arrays):
+        return [pltpu.with_memory_space_constraint(a, pltpu.VMEM) for a in arrays]
+
+    transition, proc_noise, prior_mean, prior_var = near(
+        transition, proc_noise, prior_mean[None], prior_var[None]
+    )
+    prepared = pl.pallas_call(
+        prepare,
+        out_shape=(
+            pltpu.VMEM((size + 8, size), jnp.float32),
+            pltpu.VMEM((size, size), jnp.float32),
+            pltpu.VMEM((sensors, size), jnp.float32),
+            pltpu.VMEM((1, sensors), jnp.float32),
+        ),
+        in_specs=[vmem] * 6,
+        out_specs=(vmem,) * 4,
+        name="prepare_window",
+    )(*near(sensor_map[None], obs_var[None]), transition, proc_noise, prior_mean, prior_var)
     return pl.pallas_call(
         kernel,
         out_shape=(
             jax.ShapeDtypeStruct((steps_here, size), jnp.float32),
             jax.ShapeDtypeStruct((steps_here, size, size), jnp.float32),
         ),
-        in_specs=[pl.BlockSpec(memory_space=pltpu.SMEM)] + [vmem] * 7,
+        in_specs=[pl.BlockSpec(memory_space=pltpu.SMEM)] + [vmem] * 9,
         out_specs=(vmem, vmem),
         scratch_shapes=[
             pltpu.VMEM((steps, sensors), jnp.float32),
             pltpu.VMEM((steps, sensors), jnp.float32),
             pltpu.VMEM((size, size), jnp.float32),
             pltpu.VMEM((steps, 8, size), jnp.float32),
-            pltpu.VMEM((size, size), jnp.float32),
+            pltpu.VMEM((size, size), jnp.bfloat16),
+            pltpu.VMEM((size, size), jnp.bfloat16),
         ],
         name="filter_window",
     )(
-        position.astype(jnp.int32)[None], gathered, sensor_map[None], transition, proc_noise,
-        obs_var[None], prior_mean[None], prior_var[None],
+        position.astype(jnp.int32)[None], *near(gathered, *prepared), transition, proc_noise,
+        prior_mean, prior_var,
     )
 
 

time: 23 us -> 22.1 us (0.961)
  local copies, waits for them, and re-layouts: 0.01 us -> 2.96 us
  waiting for transfers between devices: 5.28 us -> 3.01 us
  Pallas kernels: 13.2 us -> 12.1 us
  other arithmetic: 1.31 us -> 0.71 us
    unnamed x2 -> x18, local copies, waits for them, and re-layouts: 0.01 us -> 2.96 us
    ppermute x3, waiting for transfers between devices: 5.28 us -> 3.01 us  [gather_steps(): lax.ppermute(gathered, TIME_AXES, pairs)]
    pallas_call x1, Pallas kernels: 13.2 us -> 11.9 us  [local(): pl.pallas_call(kernel, out_shape=(jax.ShapeDtypeStruct((steps_here, size)...]
    concatenate x3, other arithmetic: 0.61 us -> 0.02 us  [gather_steps(): jnp.concatenate([gathered, lax.ppermute(gathered, TIME_AXES, pairs)], 0)]
    pallas_call x0 -> x1, Pallas kernels: none -> 0.26 us  [local(): pl.pallas_call(prepare, out_shape=(pltpu.VMEM((size + 8, size), jnp.float...]
  transfers between devices with their start and end apart: 3 -> 3, of which waited for: 3 -> 2; matrix products, arithmetic and copies ran while one was open for 0% -> 0% of each run, Pallas kernels for 0% -> 1%
where the time goes in v3:
time: 22.1 us; the launch traced here: 21.8 us
  Pallas kernels  12.1 us (55%)
  waiting for transfers between devices  3.01 us (14%)
  local copies, waits for them, and re-layouts  2.96 us (13%)
  starting transfers between devices  2.37 us (11%)
  other arithmetic  0.71 us (3%)
  between operations  0.67 us (3%)
    pallas_call x1, Pallas kernels, local(): pl.pallas_call(kernel, out_shape=(jax.ShapeDtypeStruct((steps_here, size)...  11.9 us
    ppermute x3, waiting for transfers between devices, gather_steps(): lax.ppermute(gathered, TIME_AXES, pairs)  3.01 us
    unnamed x18, local copies, waits for them, and re-layouts  2.96 us
    ppermute x3, starting transfers between devices, gather_steps(): lax.ppermute(gathered, TIME_AXES, pairs)  2.37 us
    convert_element_type x1, other arithmetic, local(): rows = jnp.concatenate([observations, obs_mask.astype(jnp.float32)], 0)  0.69 us
  transfers between devices with their start and end apart: 3, of which 2 were waited for; matrix products, arithmetic and copies ran while one was open for 0% of the time, Pallas kernels for 1%

profile of v3, /device:TPU:31, one launch (start us, length us, event | category | flops | bytes accessed | tf_op | source)
XLA Modules:
  0.0 21.8 jit_solution(8375716586072682886)
XLA Ops:
  0.6 0.0 copy-start.8
  0.6 0.7 %convert_element_type.3 = f32[2,128]{1,0:T(2,128)S(1)} convert(s32[2,128]{1,0:T(2,128)} %param.9) | non-fusion elementwise | flops 256 | bytes 2048 | tf_op jit(solution)/shard_map/convert_element_type | solution.py:235
  1.3 0.0 copy-done.8
  1.3 0.3 %collective-permute-start = (f32[1,4,128]{2,1,0:T(4,128)S(1)}, f32[1,4,128]{2,1,0:T(4,128)S(1)}, u32[]{:S(2)}, u32[]{:S(2)}) collective-permute-start(f32[1,4,128]{2,1,0:T(4,128)S(1)} %maximum_bitcast_fusion), channel_id=1, source_target_pairs={{0,4},{4,0},{8,12},{12,8},{16,20},{20,16},{24,28},{28,24},{1,5},{5... | collective-permute-start | bytes 6152 | tf_op jit(solution)/shard_map/ppermute | solution.py:58
  1.7 2.2 %collective-permute-done = f32[1,4,128]{2,1,0:T(4,128)S(1)} collective-permute-done((f32[1,4,128]{2,1,0:T(4,128)S(1)}, f32[1,4,128]{2,1,0:T(4,128)S(1)}, u32[]{:S(2)}, u32[]{:S(2)}) %collective-permute-start) | collective-permute-done | bytes 2080 | tf_op jit(solution)/shard_map/ppermute | solution.py:58
  3.8 1.8 %collective-permute-start.1 = (f32[2,4,128]{2,1,0:T(4,128)S(1)}, f32[2,4,128]{2,1,0:T(4,128)S(1)}, u32[]{:S(2)}, u32[]{:S(2)}) collective-permute-start(f32[2,4,128]{2,1,0:T(4,128)S(1)} %pad_maximum_fusion.2), channel_id=1, source_target_pairs={{0,8},{4,12},{8,0},{12,4},{16,24},{20,28},{24,16},{28,20},{1,9},{5... | collective-permute-start | bytes 12296 | tf_op jit(solution)/shard_map/ppermute | solution.py:58
  5.7 0.8 %collective-permute-done.1 = f32[2,4,128]{2,1,0:T(4,128)S(1)} collective-permute-done((f32[2,4,128]{2,1,0:T(4,128)S(1)}, f32[2,4,128]{2,1,0:T(4,128)S(1)}, u32[]{:S(2)}, u32[]{:S(2)}) %collective-permute-start.1) | collective-permute-done | bytes 4128 | tf_op jit(solution)/shard_map/ppermute | solution.py:58
  6.5 0.2 %collective-permute-start.2 = (f32[4,4,128]{2,1,0:T(4,128)S(1)}, f32[4,4,128]{2,1,0:T(4,128)S(1)}, u32[]{:S(2)}, u32[]{:S(2)}) collective-permute-start(f32[4,4,128]{2,1,0:T(4,128)S(1)} %pad_maximum_fusion.1), channel_id=1, source_target_pairs={{0,16},{4,20},{8,24},{12,28},{16,0},{20,4},{24,8},{28,12},{1,17},{... | collective-permute-start | bytes 24584 | tf_op jit(solution)/shard_map/ppermute | solution.py:58
  6.7 0.0 copy-start.7
  6.7 0.0 copy-start.4
  6.7 0.0 copy-start.5
  6.7 0.0 copy-start.6
  6.7 0.6 %copy-done.7 = f32[128]{0:T(128)S(1)} copy-done((f32[128]{0:T(128)S(1)}, f32[128]{0:T(128)}, u32[]{:S(2)}) %copy-start.7) | copy-done | bytes 536
  7.4 0.0 copy-done.4
  7.4 0.0 copy-done.5
  7.4 0.0 copy-done.6
  7.4 0.0 copy-start
  7.4 0.8 %copy-done = f32[128,128]{1,0:T(8,128)S(1)} copy-done((f32[128,128]{1,0:T(8,128)S(1)}, f32[128,128]{1,0:T(8,128)}, u32[]{:S(2)}) %copy-start) | copy-done | bytes 65560
  8.3 0.0 copy-start.2
  8.3 0.8 %copy-done.2 = f32[128,128]{1,0:T(8,128)S(1)} copy-done((f32[128,128]{1,0:T(8,128)S(1)}, f32[128,128]{1,0:T(8,128)}, u32[]{:S(2)}) %copy-start.2) | copy-done | bytes 65560
  9.1 0.0 copy-start.1
  9.1 0.0 copy-start.3
  9.1 0.3 %prepare_window.1 = (f32[136,128]{1,0:T(8,128)S(1)}, f32[128,128]{1,0:T(8,128)S(1)}, f32[128,128]{1,0:T(8,128)S(1)}, f32[1,128]{1,0:T(1,128)S(1)}) custom-call(s32[1,128]{1,0:T(1,128)S(1)} %bitcast.11, f32[1,128]{1,0:T(1,128)S(1)} %bitcast.12, f32[128,128]{1,0:T(8,128)S(1)} %copy-done, f32[128,128]{1,0:T(8,128)S(1)} %copy-done.2, f32[1,128]{1,0:T(1,128)S(1)} %bitcast.7, ...), custom_call_target="tpu_custom_call" | custom-call | tf_op jit(solution)/shard_map/prepare_window/pallas_call | solution.py:246
  9.4 0.0 collective-permute-done.2
  9.4 0.6 %copy-done.1 = f32[128,128]{1,0:T(8,128)S(1)} copy-done((f32[128,128]{1,0:T(8,128)S(1)}, f32[128,128]{1,0:T(8,128)}, u32[]{:S(2)}) %copy-start.1) | copy-done | bytes 65560
  9.9 0.0 copy-done.3
  10.0 11.9 %filter_window.1 = (f32[2,128]{1,0:T(2,128)}, f32[2,128,128]{2,1,0:T(8,128)}) custom-call(s32[1]{0:T(128)} %bitcast.own_ref, f32[8,4,128]{2,1,0:T(4,128)S(1)} %pad_maximum_fusion.steps_ref, f32[136,128]{1,0:T(8,128)S(1)} %get-tuple-element.6.start_ref, f32[128,128]{1,0:T(8,128)S(1)} %get-tuple-element.7.turned_ref, ...), custom_call_target="tpu_custom_call" | custom-call | tf_op jit(solution)/shard_map/filter_window/pallas_call | solution.py:258
  (4 shorter events, 0.0 us)
Async XLA Ops:
  0.6 0.7 %copy-start.8 = (f32[2,128]{1,0:T(2,128)S(1)}, f32[2,128]{1,0:T(2,128)}, u32[]{:S(2)}) copy-start(f32[2,128]{1,0:T(2,128)} %param.8) | copy-start | bytes 3076
  1.3 2.5 %collective-permute-start = (f32[1,4,128]{2,1,0:T(4,128)S(1)}, f32[1,4,128]{2,1,0:T(4,128)S(1)}, u32[]{:S(2)}, u32[]{:S(2)}) collective-permute-start(f32[1,4,128]{2,1,0:T(4,128)S(1)} %maximum_bitcast_fusion), channel_id=1, source_target_pairs={{0,4},{4,0},{8,12},{12,8},{16,20},{20,16},{24,28},{28,24},{1,5},{5... | collective-permute-start | bytes 6152 | tf_op jit(solution)/shard_map/ppermute | solution.py:58
  3.8 2.6 %collective-permute-start.1 = (f32[2,4,128]{2,1,0:T(4,128)S(1)}, f32[2,4,128]{2,1,0:T(4,128)S(1)}, u32[]{:S(2)}, u32[]{:S(2)}) collective-permute-start(f32[2,4,128]{2,1,0:T(4,128)S(1)} %pad_maximum_fusion.2), channel_id=1, source_target_pairs={{0,8},{4,12},{8,0},{12,4},{16,24},{20,28},{24,16},{28,20},{1,9},{5... | collective-permute-start | bytes 12296 | tf_op jit(solution)/shard_map/ppermute | solution.py:58
  6.5 2.9 %collective-permute-start.2 = (f32[4,4,128]{2,1,0:T(4,128)S(1)}, f32[4,4,128]{2,1,0:T(4,128)S(1)}, u32[]{:S(2)}, u32[]{:S(2)}) collective-permute-start(f32[4,4,128]{2,1,0:T(4,128)S(1)} %pad_maximum_fusion.1), channel_id=1, source_target_pairs={{0,16},{4,20},{8,24},{12,28},{16,0},{20,4},{24,8},{28,12},{1,17},{... | collective-permute-start | bytes 24584 | tf_op jit(solution)/shard_map/ppermute | solution.py:58
  6.7 0.7 %copy-start.7 = (f32[128]{0:T(128)S(1)}, f32[128]{0:T(128)}, u32[]{:S(2)}) copy-start(f32[128]{0:T(128)} %param.13) | copy-start | bytes 1540
  6.7 0.7 %copy-start.4 = (f32[128]{0:T(128)S(1)}, f32[128]{0:T(128)}, u32[]{:S(2)}) copy-start(f32[128]{0:T(128)} %param.14) | copy-start | bytes 1540
  6.7 0.7 %copy-start.5 = (f32[128]{0:T(128)S(1)}, f32[128]{0:T(128)}, u32[]{:S(2)}) copy-start(f32[128]{0:T(128)} %param.15) | copy-start | bytes 1540
  6.7 0.7 %copy-start.6 = (s32[128]{0:T(128)S(1)}, s32[128]{0:T(128)}, u32[]{:S(2)}) copy-start(s32[128]{0:T(128)} %param.10) | copy-start | bytes 1540
  7.4 0.8 %copy-start = (f32[128,128]{1,0:T(8,128)S(1)}, f32[128,128]{1,0:T(8,128)}, u32[]{:S(2)}) copy-start(f32[128,128]{1,0:T(8,128)} %trans_ref.3) | copy-start | bytes 196612
  8.3 0.8 %copy-start.2 = (f32[128,128]{1,0:T(8,128)S(1)}, f32[128,128]{1,0:T(8,128)}, u32[]{:S(2)}) copy-start(f32[128,128]{1,0:T(8,128)} %noise_ref.3) | copy-start | bytes 196612
  9.1 0.8 %copy-start.1 = (f32[128,128]{1,0:T(8,128)S(1)}, f32[128,128]{1,0:T(8,128)}, u32[]{:S(2)}) copy-start(f32[128,128]{1,0:T(8,128)} %trans_ref.3) | copy-start | bytes 196612
  9.1 0.9 %copy-start.3 = (f32[128,128]{1,0:T(8,128)S(1)}, f32[128,128]{1,0:T(8,128)}, u32[]{:S(2)}) copy-start(f32[128,128]{1,0:T(8,128)} %noise_ref.3) | copy-start | bytes 196612

commit v4 on v3

--- a/solution.py
+++ b/solution.py
@@ -62,7 +62,7 @@
 
 def prepare(
     map_ref, var_ref, trans_ref, noise_ref, mean_ref, prior_ref,
-    start_ref, turned_ref, chosen_ref, inv_var_ref,
+    start_ref, turned_ref, chosen_ref, inv_var_ref, trans_out, noise_out, mean_out, prior_out,
 ):
     size = trans_ref.shape[0]
     sensors = map_ref.shape[1]
@@ -79,6 +79,10 @@
     chosen = (components == map_ref[...]).astype(jnp.float32)
     chosen_ref[...] = chosen.T
     inv_var_ref[...] = 1.0 / var_ref[...]
+    trans_out[...] = trans
+    noise_out[...] = noise_ref[...]
+    mean_out[...] = mean_ref[...]
+    prior_out[...] = prior_ref[...]
 
 
 def kernel(
@@ -240,9 +244,6 @@
     def near(*arrays):
         return [pltpu.with_memory_space_constraint(a, pltpu.VMEM) for a in arrays]
 
-    transition, proc_noise, prior_mean, prior_var = near(
-        transition, proc_noise, prior_mean[None], prior_var[None]
-    )
     prepared = pl.pallas_call(
         prepare,
         out_shape=(
@@ -250,11 +251,15 @@
             pltpu.VMEM((size, size), jnp.float32),
             pltpu.VMEM((sensors, size), jnp.float32),
             pltpu.VMEM((1, sensors), jnp.float32),
+            pltpu.VMEM((size, size), jnp.float32),
+            pltpu.VMEM((size, size), jnp.float32),
+            pltpu.VMEM((1, size), jnp.float32),
+            pltpu.VMEM((1, size), jnp.float32),
         ),
         in_specs=[vmem] * 6,
-        out_specs=(vmem,) * 4,
+        out_specs=(vmem,) * 8,
         name="prepare_window",
-    )(*near(sensor_map[None], obs_var[None]), transition, proc_noise, prior_mean, prior_var)
+    )(sensor_map[None], obs_var[None], transition, proc_noise, prior_mean[None], prior_var[None])
     return pl.pallas_call(
         kernel,
         out_shape=(
@@ -273,8 +278,7 @@
         ],
         name="filter_window",
     )(
-        position.astype(jnp.int32)[None], *near(gathered, *prepared), transition, proc_noise,
-        prior_mean, prior_var,
+        position.astype(jnp.int32)[None], *near(gathered, *prepared)
     )
 
 

time: 22.1 us -> 21.1 us (0.955)
  local copies, waits for them, and re-layouts: 2.96 us -> 0.01 us
  waiting for transfers between devices: 3.01 us -> 4.11 us
  Pallas kernels: 12.1 us -> 13 us
    unnamed x18 -> x2, local copies, waits for them, and re-layouts: 2.96 us -> 0.01 us
    ppermute x3, waiting for transfers between devices: 3.01 us -> 4.11 us  [gather_steps(): lax.ppermute(gathered, TIME_AXES, pairs)]
    pallas_call x1, Pallas kernels: 0.26 us -> 1.16 us  [local(): pl.pallas_call(prepare, out_shape=(pltpu.VMEM((size + 8, size), jnp.float...]
  transfers between devices with their start and end apart: 3 -> 3, of which waited for: 2 -> 3; matrix products, arithmetic and copies ran while one was open for 0% -> 0% of each run, Pallas kernels for 1% -> 6%
where the time goes in v4:
time: 21.1 us; the launch traced here: 20.9 us
  Pallas kernels  13 us (62%)
  waiting for transfers between devices  4.11 us (19%)
  starting transfers between devices  2.37 us (11%)
  other arithmetic  0.71 us (3%)
  between operations  0.65 us (3%)
    pallas_call x1, Pallas kernels, local(): pl.pallas_call(kernel, out_shape=(jax.ShapeDtypeStruct((steps_here, size)...  11.9 us
    ppermute x3, waiting for transfers between devices, gather_steps(): lax.ppermute(gathered, TIME_AXES, pairs)  4.11 us
    ppermute x3, starting transfers between devices, gather_steps(): lax.ppermute(gathered, TIME_AXES, pairs)  2.37 us
    pallas_call x1, Pallas kernels, local(): pl.pallas_call(prepare, out_shape=(pltpu.VMEM((size + 8, size), jnp.float...  1.16 us
    convert_element_type x1, other arithmetic, local(): rows = jnp.concatenate([observations, obs_mask.astype(jnp.float32)], 0)  0.69 us
  transfers between devices with their start and end apart: 3, of which 3 were waited for; matrix products, arithmetic and copies ran while one was open for 0% of the time, Pallas kernels for 6%

profile of v4, /device:TPU:31, one launch (start us, length us, event | category | flops | bytes accessed | tf_op | source)
XLA Modules:
  0.0 20.9 jit_solution(5086274768430876026)
XLA Ops:
  0.6 0.0 copy-start
  0.6 0.7 %convert_element_type.3 = f32[2,128]{1,0:T(2,128)S(1)} convert(s32[2,128]{1,0:T(2,128)} %param.9) | non-fusion elementwise | flops 256 | bytes 2048 | tf_op jit(solution)/shard_map/convert_element_type | solution.py:239
  1.3 0.0 copy-done
  1.3 0.3 %collective-permute-start = (f32[1,4,128]{2,1,0:T(4,128)S(1)}, f32[1,4,128]{2,1,0:T(4,128)S(1)}, u32[]{:S(2)}, u32[]{:S(2)}) collective-permute-start(f32[1,4,128]{2,1,0:T(4,128)S(1)} %maximum_bitcast_fusion), channel_id=1, source_target_pairs={{0,4},{4,0},{8,12},{12,8},{16,20},{20,16},{24,28},{28,24},{1,5},{5... | collective-permute-start | bytes 6152 | tf_op jit(solution)/shard_map/ppermute | solution.py:58
  1.7 2.2 %collective-permute-done = f32[1,4,128]{2,1,0:T(4,128)S(1)} collective-permute-done((f32[1,4,128]{2,1,0:T(4,128)S(1)}, f32[1,4,128]{2,1,0:T(4,128)S(1)}, u32[]{:S(2)}, u32[]{:S(2)}) %collective-permute-start) | collective-permute-done | bytes 2080 | tf_op jit(solution)/shard_map/ppermute | solution.py:58
  3.8 1.8 %collective-permute-start.1 = (f32[2,4,128]{2,1,0:T(4,128)S(1)}, f32[2,4,128]{2,1,0:T(4,128)S(1)}, u32[]{:S(2)}, u32[]{:S(2)}) collective-permute-start(f32[2,4,128]{2,1,0:T(4,128)S(1)} %pad_maximum_fusion.2), channel_id=1, source_target_pairs={{0,8},{4,12},{8,0},{12,4},{16,24},{20,28},{24,16},{28,20},{1,9},{5... | collective-permute-start | bytes 12296 | tf_op jit(solution)/shard_map/ppermute | solution.py:58
  5.7 0.8 %collective-permute-done.1 = f32[2,4,128]{2,1,0:T(4,128)S(1)} collective-permute-done((f32[2,4,128]{2,1,0:T(4,128)S(1)}, f32[2,4,128]{2,1,0:T(4,128)S(1)}, u32[]{:S(2)}, u32[]{:S(2)}) %collective-permute-start.1) | collective-permute-done | bytes 4128 | tf_op jit(solution)/shard_map/ppermute | solution.py:58
  6.5 0.2 %collective-permute-start.2 = (f32[4,4,128]{2,1,0:T(4,128)S(1)}, f32[4,4,128]{2,1,0:T(4,128)S(1)}, u32[]{:S(2)}, u32[]{:S(2)}) collective-permute-start(f32[4,4,128]{2,1,0:T(4,128)S(1)} %pad_maximum_fusion.1), channel_id=1, source_target_pairs={{0,16},{4,20},{8,24},{12,28},{16,0},{20,4},{24,8},{28,12},{1,17},{... | collective-permute-start | bytes 24584 | tf_op jit(solution)/shard_map/ppermute | solution.py:58
  6.7 1.2 %prepare_window.1 = (f32[136,128]{1,0:T(8,128)S(1)}, f32[128,128]{1,0:T(8,128)S(1)}, f32[128,128]{1,0:T(8,128)S(1)}, f32[1,128]{1,0:T(1,128)S(1)}, f32[128,128]{...) custom-call(s32[1,128]{1,0:T(1,128)} %bitcast.7, f32[1,128]{1,0:T(1,128)} %bitcast.8, ...), custom_call_target="tpu_custom_call" | custom-call | tf_op jit(solution)/shard_map/prepare_window/pallas_call | solution.py:247
  7.9 1.1 %collective-permute-done.2 = f32[4,4,128]{2,1,0:T(4,128)S(1)} collective-permute-done((f32[4,4,128]{2,1,0:T(4,128)S(1)}, f32[4,4,128]{2,1,0:T(4,128)S(1)}, u32[]{:S(2)}, u32[]{:S(2)}) %collective-permute-start.2) | collective-permute-done | bytes 8224 | tf_op jit(solution)/shard_map/ppermute | solution.py:58
  9.0 11.9 %filter_window.1 = (f32[2,128]{1,0:T(2,128)}, f32[2,128,128]{2,1,0:T(8,128)}) custom-call(s32[1]{0:T(128)} %bitcast.own_ref, f32[8,4,128]{2,1,0:T(4,128)S(1)} %pad_maximum_fusion.steps_ref, f32[136,128]{1,0:T(8,128)S(1)} %get-tuple-element.10.start_ref, f32[128,128]{1,0:T(8,128)S(1)} %get-tuple-element.11.turned_ref, ...), custom_call_target="tpu_custom_call" | custom-call | tf_op jit(solution)/shard_map/filter_window/pallas_call | solution.py:263
  (4 shorter events, 0.0 us)
Async XLA Ops:
  0.6 0.7 %copy-start = (f32[2,128]{1,0:T(2,128)S(1)}, f32[2,128]{1,0:T(2,128)}, u32[]{:S(2)}) copy-start(f32[2,128]{1,0:T(2,128)} %param.8) | copy-start | bytes 3076
  1.3 2.5 %collective-permute-start = (f32[1,4,128]{2,1,0:T(4,128)S(1)}, f32[1,4,128]{2,1,0:T(4,128)S(1)}, u32[]{:S(2)}, u32[]{:S(2)}) collective-permute-start(f32[1,4,128]{2,1,0:T(4,128)S(1)} %maximum_bitcast_fusion), channel_id=1, source_target_pairs={{0,4},{4,0},{8,12},{12,8},{16,20},{20,16},{24,28},{28,24},{1,5},{5... | collective-permute-start | bytes 6152 | tf_op jit(solution)/shard_map/ppermute | solution.py:58
  3.8 2.6 %collective-permute-start.1 = (f32[2,4,128]{2,1,0:T(4,128)S(1)}, f32[2,4,128]{2,1,0:T(4,128)S(1)}, u32[]{:S(2)}, u32[]{:S(2)}) collective-permute-start(f32[2,4,128]{2,1,0:T(4,128)S(1)} %pad_maximum_fusion.2), channel_id=1, source_target_pairs={{0,8},{4,12},{8,0},{12,4},{16,24},{20,28},{24,16},{28,20},{1,9},{5... | collective-permute-start | bytes 12296 | tf_op jit(solution)/shard_map/ppermute | solution.py:58
  6.5 2.5 %collective-permute-start.2 = (f32[4,4,128]{2,1,0:T(4,128)S(1)}, f32[4,4,128]{2,1,0:T(4,128)S(1)}, u32[]{:S(2)}, u32[]{:S(2)}) collective-permute-start(f32[4,4,128]{2,1,0:T(4,128)S(1)} %pad_maximum_fusion.1), channel_id=1, source_target_pairs={{0,16},{4,20},{8,24},{12,28},{16,0},{20,4},{24,8},{28,12},{1,17},{... | collective-permute-start | bytes 24584 | tf_op jit(solution)/shard_map/ppermute | solution.py:58

commit v5 on v4

--- a/solution.py
+++ b/solution.py
@@ -1,3 +1,4 @@
+import functools
 import math
 
 import jax
@@ -50,18 +51,31 @@
     )
 
 
-def gather_steps(rows, parts):
+def exchange_order(outer, inner):
+    bits = (outer * inner).bit_length() - 1
+    core = inner.bit_length() - 1
+    return [core] + [b for b in range(bits) if b != core]
+
+
+def gather_steps(rows, order):
+    parts = 1 << len(order)
     gathered = rows[None]
-    reach = 1
-    while reach < parts:
-        pairs = [(i, i ^ reach) for i in range(parts)]
-        gathered = jnp.concatenate([gathered, lax.ppermute(gathered, TIME_AXES, pairs)], 0)
-        reach *= 2
-    return gathered
+
+    def from_across(mask):
+        return lax.ppermute(gathered, TIME_AXES, [(i, i ^ mask) for i in range(parts)])
+
+    stages = []
+    for bits in [order[:1]] + [order[i : i + 2] for i in range(1, len(order), 2)]:
+        masks = [0]
+        for bit in bits:
+            masks += [m | 1 << bit for m in masks]
+        gathered = jnp.concatenate([gathered] + [from_across(m) for m in masks[1:]], 0)
+        stages.append(gathered)
+    return stages
 
 
 def prepare(
-    map_ref, var_ref, trans_ref, noise_ref, mean_ref, prior_ref,
+    after_ref, map_ref, var_ref, trans_ref, noise_ref, mean_ref, prior_ref,
     start_ref, turned_ref, chosen_ref, inv_var_ref, trans_out, noise_out, mean_out, prior_out,
 ):
     size = trans_ref.shape[0]
@@ -88,7 +102,7 @@
 def kernel(
     own_ref, steps_ref, start_ref, turned_ref, chosen_ref, inv_var_ref, trans_ref, noise_ref,
     mean_ref, prior_ref, mean_out, cov_out, prec_ref, info_ref, state_ref, check_ref, high_ref,
-    low_ref,
+    low_ref, *, order,
 ):
     parts, rows_each, width = steps_ref.shape
     per_part = rows_each // 2
@@ -103,7 +117,9 @@
     inv_var = inv_var_ref[...]
 
     def place(source, carried):
-        block = steps_ref[source ^ own]
+        mask = source ^ own
+        slot = sum(((mask >> bit) & 1) << i for i, bit in enumerate(order))
+        block = steps_ref[slot]
         weight = block[per_part:] * inv_var
         prec_ref[pl.ds(source * per_part, per_part), :] = weight
         info_ref[pl.ds(source * per_part, per_part), :] = weight * block[:per_part]
@@ -235,9 +251,11 @@
     steps_here, sensors = observations.shape
     size = transition.shape[0]
     parts = lax.axis_size("outer") * lax.axis_size("inner")
+    order = exchange_order(lax.axis_size("outer"), lax.axis_size("inner"))
     position = lax.axis_index("outer") * lax.axis_size("inner") + lax.axis_index("inner")
     rows = jnp.concatenate([observations, obs_mask.astype(jnp.float32)], 0)
-    gathered = gather_steps(rows, parts)
+    stages = gather_steps(rows, order)
+    gathered = stages[-1]
     steps = parts * steps_here
     vmem = pl.BlockSpec(memory_space=pltpu.VMEM)
 
@@ -256,12 +274,12 @@
             pltpu.VMEM((1, size), jnp.float32),
             pltpu.VMEM((1, size), jnp.float32),
         ),
-        in_specs=[vmem] * 6,
+        in_specs=[vmem] * 7,
         out_specs=(vmem,) * 8,
         name="prepare_window",
-    )(sensor_map[None], obs_var[None], transition, proc_noise, prior_mean[None], prior_var[None])
+    )(*near(stages[0]), sensor_map[None], obs_var[None], transition, proc_noise, prior_mean[None], prior_var[None])
     return pl.pallas_call(
-        kernel,
+        functools.partial(kernel, order=order),
         out_shape=(
             jax.ShapeDtypeStruct((steps_here, size), jnp.float32),
             jax.ShapeDtypeStruct((steps_here, size, size), jnp.float32),

time: 21.1 us -> 19.2 us (0.910)
  waiting for transfers between devices: 4.11 us -> 1.18 us
  starting transfers between devices: 2.37 us -> 3.39 us
    ppermute x3 -> x4, waiting for transfers between devices: 4.11 us -> 1.18 us  [from_across(): lax.ppermute(gathered, TIME_AXES, [(i, i ^ mask) for i in range(parts)])]
    ppermute x3 -> x4, starting transfers between devices: 2.37 us -> 3.39 us  [from_across(): lax.ppermute(gathered, TIME_AXES, [(i, i ^ mask) for i in range(parts)])]
  transfers between devices with their start and end apart: 3 -> 4, of which waited for: 3 -> 2; matrix products, arithmetic and copies ran while one was open for 0% -> 0% of each run, Pallas kernels for 6% -> 6%
where the time goes in v5:
time: 19.2 us; the launch traced here: 19 us
  Pallas kernels  13.1 us (68%)
  starting transfers between devices  3.39 us (18%)
  waiting for transfers between devices  1.18 us (6%)
  other arithmetic  0.71 us (4%)
  between operations  0.65 us (3%)
    pallas_call x1, Pallas kernels, local(): pl.pallas_call(functools.partial(kernel, order=order), out_shape=(jax.Sha...  11.9 us
    ppermute x4, starting transfers between devices, from_across(): lax.ppermute(gathered, TIME_AXES, [(i, i ^ mask) for i in range(parts)])  3.39 us
    ppermute x4, waiting for transfers between devices, from_across(): lax.ppermute(gathered, TIME_AXES, [(i, i ^ mask) for i in range(parts)])  1.18 us
    pallas_call x1, Pallas kernels, local(): pl.pallas_call(prepare, out_shape=(pltpu.VMEM((size + 8, size), jnp.float...  1.17 us
    convert_element_type x1, other arithmetic, local(): rows = jnp.concatenate([observations, obs_mask.astype(jnp.float32)], 0)  0.69 us
  transfers between devices with their start and end apart: 4, of which 2 were waited for; matrix products, arithmetic and copies ran while one was open for 0% of the time, Pallas kernels for 6%

profile of v5, /device:TPU:31, one launch (start us, length us, event | category | flops | bytes accessed | tf_op | source)
XLA Modules:
  0.0 19.0 jit_solution(5789082812083677719)
XLA Ops:
  0.6 0.0 copy-start
  0.6 0.7 %convert_element_type.3 = f32[2,128]{1,0:T(2,128)S(1)} convert(s32[2,128]{1,0:T(2,128)} %param.9) | non-fusion elementwise | flops 256 | bytes 2048 | tf_op jit(solution)/shard_map/convert_element_type | solution.py:256
  1.3 0.0 copy-done
  1.3 0.7 %collective-permute-start = (f32[1,4,128]{2,1,0:T(4,128)S(1)}, f32[1,4,128]{2,1,0:T(4,128)S(1)}, u32[]{:S(2)}, u32[]{:S(2)}) collective-permute-start(f32[1,4,128]{2,1,0:T(4,128)S(1)} %maximum_bitcast_fusion), channel_id=1, source_target_pairs={{0,8},{4,12},{8,0},{12,4},{16,24},{20,28},{24,16},{28,20},{1,9},{5... | collective-permute-start | bytes 6152 | tf_op jit(solution)/shard_map/ppermute | solution.py:65
  2.1 0.8 %collective-permute-done = f32[1,4,128]{2,1,0:T(4,128)S(1)} collective-permute-done((f32[1,4,128]{2,1,0:T(4,128)S(1)}, f32[1,4,128]{2,1,0:T(4,128)S(1)}, u32[]{:S(2)}, u32[]{:S(2)}) %collective-permute-start) | collective-permute-done | bytes 2080 | tf_op jit(solution)/shard_map/ppermute | solution.py:65
  2.9 0.2 %collective-permute-start.3 = (f32[2,4,128]{2,1,0:T(4,128)S(1)}, f32[2,4,128]{2,1,0:T(4,128)S(1)}, u32[]{:S(2)}, u32[]{:S(2)}) collective-permute-start(f32[2,4,128]{2,1,0:T(4,128)S(1)} %pad_maximum_fusion.after_ref), channel_id=1, source_target_pairs={{0,20},{4,16},{8,28},{12,24},{16,4},{20,0},{24,12},{28,8},{1,21},{... | collective-permute-start | bytes 12296 | tf_op jit(solution)/shard_map/ppermute | solution.py:65
  3.1 1.2 %collective-permute-start.2 = (f32[2,4,128]{2,1,0:T(4,128)S(1)}, f32[2,4,128]{2,1,0:T(4,128)S(1)}, u32[]{:S(2)}, u32[]{:S(2)}) collective-permute-start(f32[2,4,128]{2,1,0:T(4,128)S(1)} %pad_maximum_fusion.after_ref), channel_id=1, source_target_pairs={{0,16},{4,20},{8,24},{12,28},{16,0},{20,4},{24,8},{28,12},{1,17},{... | collective-permute-start | bytes 12296 | tf_op jit(solution)/shard_map/ppermute | solution.py:65
  4.3 1.2 %collective-permute-start.1 = (f32[2,4,128]{2,1,0:T(4,128)S(1)}, f32[2,4,128]{2,1,0:T(4,128)S(1)}, u32[]{:S(2)}, u32[]{:S(2)}) collective-permute-start(f32[2,4,128]{2,1,0:T(4,128)S(1)} %pad_maximum_fusion.after_ref), channel_id=1, source_target_pairs={{0,4},{4,0},{8,12},{12,8},{16,20},{20,16},{24,28},{28,24},{1,5},{5... | collective-permute-start | bytes 12296 | tf_op jit(solution)/shard_map/ppermute | solution.py:65
  5.6 1.2 %prepare_window.1 = (f32[136,128]{1,0:T(8,128)S(1)}, f32[128,128]{1,0:T(8,128)S(1)}, f32[128,128]{1,0:T(8,128)S(1)}, f32[1,128]{1,0:T(1,128)S(1)}, f32[128,128]{...) custom-call(f32[2,4,128]{2,1,0:T(4,128)S(1)} %pad_maximum_fusion.after_ref, ...), custom_call_target="tpu_custom_call" | custom-call | tf_op jit(solution)/shard_map/prepare_window/pallas_call | solution.py:265
  6.7 0.4 %collective-permute-done.1 = f32[2,4,128]{2,1,0:T(4,128)S(1)} collective-permute-done((f32[2,4,128]{2,1,0:T(4,128)S(1)}, f32[2,4,128]{2,1,0:T(4,128)S(1)}, u32[]{:S(2)}, u32[]{:S(2)}) %collective-permute-start.1) | collective-permute-done | bytes 4128 | tf_op jit(solution)/shard_map/ppermute | solution.py:65
  7.1 0.0 collective-permute-done.2
  7.1 0.0 collective-permute-done.3
  7.1 11.9 %filter_window.1 = (f32[2,128]{1,0:T(2,128)}, f32[2,128,128]{2,1,0:T(8,128)}) custom-call(s32[1]{0:T(128)} %bitcast.own_ref, f32[8,4,128]{2,1,0:T(4,128)S(1)} %constant_dynamic-update-slice_fusion.steps_ref, f32[136,128]{1,0:T(8,128)S(1)} %get-tuple-element.10.start_ref, f32[128,128]{1,0:T(8,128)S(1)} %get-tuple-element.11.turned_ref, ...), custom_call_target="tpu_custom_call" | custom-call | tf_op jit(solution)/shard_map/filter_window/pallas_call | solution.py:281
  (7 shorter events, 0.1 us)
Async XLA Ops:
  0.6 0.7 %copy-start = (f32[2,128]{1,0:T(2,128)S(1)}, f32[2,128]{1,0:T(2,128)}, u32[]{:S(2)}) copy-start(f32[2,128]{1,0:T(2,128)} %param.8) | copy-start | bytes 3076
  1.3 1.6 %collective-permute-start = (f32[1,4,128]{2,1,0:T(4,128)S(1)}, f32[1,4,128]{2,1,0:T(4,128)S(1)}, u32[]{:S(2)}, u32[]{:S(2)}) collective-permute-start(f32[1,4,128]{2,1,0:T(4,128)S(1)} %maximum_bitcast_fusion), channel_id=1, source_target_pairs={{0,8},{4,12},{8,0},{12,4},{16,24},{20,28},{24,16},{28,20},{1,9},{5... | collective-permute-start | bytes 6152 | tf_op jit(solution)/shard_map/ppermute | solution.py:65
  2.9 4.2 %collective-permute-start.3 = (f32[2,4,128]{2,1,0:T(4,128)S(1)}, f32[2,4,128]{2,1,0:T(4,128)S(1)}, u32[]{:S(2)}, u32[]{:S(2)}) collective-permute-start(f32[2,4,128]{2,1,0:T(4,128)S(1)} %pad_maximum_fusion.after_ref), channel_id=1, source_target_pairs={{0,20},{4,16},{8,28},{12,24},{16,4},{20,0},{24,12},{28,8},{1,21},{... | collective-permute-start | bytes 12296 | tf_op jit(solution)/shard_map/ppermute | solution.py:65
  3.1 4.0 %collective-permute-start.2 = (f32[2,4,128]{2,1,0:T(4,128)S(1)}, f32[2,4,128]{2,1,0:T(4,128)S(1)}, u32[]{:S(2)}, u32[]{:S(2)}) collective-permute-start(f32[2,4,128]{2,1,0:T(4,128)S(1)} %pad_maximum_fusion.after_ref), channel_id=1, source_target_pairs={{0,16},{4,20},{8,24},{12,28},{16,0},{20,4},{24,8},{28,12},{1,17},{... | collective-permute-start | bytes 12296 | tf_op jit(solution)/shard_map/ppermute | solution.py:65
  4.3 2.8 %collective-permute-start.1 = (f32[2,4,128]{2,1,0:T(4,128)S(1)}, f32[2,4,128]{2,1,0:T(4,128)S(1)}, u32[]{:S(2)}, u32[]{:S(2)}) collective-permute-start(f32[2,4,128]{2,1,0:T(4,128)S(1)} %pad_maximum_fusion.after_ref), channel_id=1, source_target_pairs={{0,4},{4,0},{8,12},{12,8},{16,20},{20,16},{24,28},{28,24},{1,5},{5... | collective-permute-start | bytes 12296 | tf_op jit(solution)/shard_map/ppermute | solution.py:65

commit v6 on v4

--- a/solution.py
+++ b/solution.py
@@ -1,3 +1,4 @@
+import functools
 import math
 
 import jax
@@ -50,20 +51,53 @@
     )
 
 
-def gather_steps(rows, parts):
-    gathered = rows[None]
-    reach = 1
-    while reach < parts:
-        pairs = [(i, i ^ reach) for i in range(parts)]
-        gathered = jnp.concatenate([gathered, lax.ppermute(gathered, TIME_AXES, pairs)], 0)
-        reach *= 2
+def exchange_stages(outer, inner):
+    core = inner.bit_length() - 1
+    others = [b for b in range((outer * inner).bit_length() - 1) if b != core]
+    return [(core,)] + [tuple(others[i : i + 2]) for i in range(0, len(others), 2)]
+
+
+def slot_of(mask, stages):
+    slot, place = 0, 0
+    for stage in stages:
+        bits = [(mask >> b) & 1 for b in stage]
+        if len(bits) == 2:
+            bits[1] = bits[0] ^ bits[1]
+        for bit in bits:
+            slot = slot + (bit << place)
+            place += 1
+    return slot
+
+
+def gather_steps(own_rows, observations, obs_mask, stages):
+    parts = 1 << sum(len(stage) for stage in stages)
+
+    def across(value, mask):
+        return lax.ppermute(value, TIME_AXES, [(i, i ^ mask) for i in range(parts)])
+
+    mask = 1 << stages[0][0]
+    gathered = jnp.stack(
+        [
+            own_rows,
+            jnp.concatenate(
+                [across(observations, mask), across(obs_mask, mask).astype(jnp.float32)], 0
+            ),
+        ],
+        0,
+    )
+    for stage in stages[1:]:
+        masks = [1 << b for b in stage]
+        if len(masks) == 2:
+            masks = [masks[0] | masks[1], masks[1], masks[0]]
+        gathered = jnp.concatenate([gathered] + [across(gathered, m) for m in masks], 0)
     return gathered
 
 
 def prepare(
-    map_ref, var_ref, trans_ref, noise_ref, mean_ref, prior_ref,
-    start_ref, turned_ref, chosen_ref, inv_var_ref, trans_out, noise_out, mean_out, prior_out,
+    read_ref, mask_ref, map_ref, var_ref, trans_ref, noise_ref, mean_ref, prior_ref,
+    start_ref, turned_ref, chosen_ref, inv_var_ref, trans_out, noise_out, mean_out, prior_out, rows_out,
 ):
+    rows_out[...] = jnp.concatenate([read_ref[...], mask_ref[...].astype(jnp.float32)], 0)
     size = trans_ref.shape[0]
     sensors = map_ref.shape[1]
     trans = trans_ref[...]
@@ -86,15 +120,15 @@
 
 
 def kernel(
-    own_ref, steps_ref, start_ref, turned_ref, chosen_ref, inv_var_ref, trans_ref, noise_ref,
+    steps_ref, start_ref, turned_ref, chosen_ref, inv_var_ref, trans_ref, noise_ref,
     mean_ref, prior_ref, mean_out, cov_out, prec_ref, info_ref, state_ref, check_ref, high_ref,
-    low_ref,
+    low_ref, *, stages,
 ):
     parts, rows_each, width = steps_ref.shape
     per_part = rows_each // 2
     steps = parts * per_part
     size = trans_ref.shape[0]
-    own = own_ref[0]
+    own = lax.axis_index("outer") * lax.axis_size("inner") + lax.axis_index("inner")
     first = own * per_part
     row_ids = lax.broadcasted_iota(jnp.int32, (size, size), 0)
     col_ids = lax.broadcasted_iota(jnp.int32, (size, size), 1)
@@ -103,7 +137,7 @@
     inv_var = inv_var_ref[...]
 
     def place(source, carried):
-        block = steps_ref[source ^ own]
+        block = steps_ref[slot_of(source ^ own, stages)]
         weight = block[per_part:] * inv_var
         prec_ref[pl.ds(source * per_part, per_part), :] = weight
         info_ref[pl.ds(source * per_part, per_part), :] = weight * block[:per_part]
@@ -235,16 +269,14 @@
     steps_here, sensors = observations.shape
     size = transition.shape[0]
     parts = lax.axis_size("outer") * lax.axis_size("inner")
-    position = lax.axis_index("outer") * lax.axis_size("inner") + lax.axis_index("inner")
-    rows = jnp.concatenate([observations, obs_mask.astype(jnp.float32)], 0)
-    gathered = gather_steps(rows, parts)
+    stages = exchange_stages(lax.axis_size("outer"), lax.axis_size("inner"))
     steps = parts * steps_here
     vmem = pl.BlockSpec(memory_space=pltpu.VMEM)
 
     def near(*arrays):
         return [pltpu.with_memory_space_constraint(a, pltpu.VMEM) for a in arrays]
 
-    prepared = pl.pallas_call(
+    *prepared, own_rows = pl.pallas_call(
         prepare,
         out_shape=(
             pltpu.VMEM((size + 8, size), jnp.float32),
@@ -255,18 +287,23 @@
             pltpu.VMEM((size, size), jnp.float32),
             pltpu.VMEM((1, size), jnp.float32),
             pltpu.VMEM((1, size), jnp.float32),
+            pltpu.VMEM((2 * steps_here, sensors), jnp.float32),
         ),
-        in_specs=[vmem] * 6,
-        out_specs=(vmem,) * 8,
+        in_specs=[vmem] * 8,
+        out_specs=(vmem,) * 9,
         name="prepare_window",
-    )(sensor_map[None], obs_var[None], transition, proc_noise, prior_mean[None], prior_var[None])
+    )(
+        observations, obs_mask, sensor_map[None], obs_var[None], transition, proc_noise,
+        prior_mean[None], prior_var[None],
+    )
+    gathered = gather_steps(own_rows, observations, obs_mask, stages)
     return pl.pallas_call(
-        kernel,
+        functools.partial(kernel, stages=stages),
         out_shape=(
             jax.ShapeDtypeStruct((steps_here, size), jnp.float32),
             jax.ShapeDtypeStruct((steps_here, size, size), jnp.float32),
         ),
-        in_specs=[pl.BlockSpec(memory_space=pltpu.SMEM)] + [vmem] * 9,
+        in_specs=[vmem] * 9,
         out_specs=(vmem, vmem),
         scratch_shapes=[
             pltpu.VMEM((steps, sensors), jnp.float32),
@@ -278,7 +315,7 @@
         ],
         name="filter_window",
     )(
-        position.astype(jnp.int32)[None], *near(gathered, *prepared)
+        *near(gathered, *prepared)
     )
 
 

time: 21.1 us -> 18.8 us (0.89)
  waiting for transfers between devices: 4.11 us -> 1.3 us
  starting transfers between devices: 2.37 us -> 3.53 us
  other arithmetic: 0.71 us -> 0.03 us
    ppermute x3 -> x5, waiting for transfers between devices: 4.11 us -> 1.3 us  [across(): return lax.ppermute(value, TIME_AXES, [(i, i ^ mask) for i in range(parts)])]
    ppermute x3 -> x5, starting transfers between devices: 2.37 us -> 3.53 us  [across(): return lax.ppermute(value, TIME_AXES, [(i, i ^ mask) for i in range(parts)])]
    convert_element_type x1, other arithmetic: 0.69 us -> 0.01 us  [gather_steps(): across(obs_mask, mask).astype(jnp.float32)]
  transfers between devices with their start and end apart: 3 -> 5, of which waited for: 3 -> 2; matrix products, arithmetic and copies ran while one was open for 0% -> 0% of each run, Pallas kernels for 6% -> 6%
where the time goes in v6:
time: 18.8 us; the launch traced here: 18.6 us
  Pallas kernels  13.1 us (70%)
  starting transfers between devices  3.53 us (19%)
  waiting for transfers between devices  1.3 us (7%)
  between operations  0.66 us (4%)
    pallas_call x1, Pallas kernels, local(): pl.pallas_call(functools.partial(kernel, stages=stages), out_shape=(jax.S...  11.9 us
    ppermute x5, starting transfers between devices, across(): return lax.ppermute(value, TIME_AXES, [(i, i ^ mask) for i in range(parts)])  3.53 us
    ppermute x5, waiting for transfers between devices, across(): return lax.ppermute(value, TIME_AXES, [(i, i ^ mask) for i in range(parts)])  1.3 us
    pallas_call x1, Pallas kernels, local(): pl.pallas_call(prepare, out_shape=(pltpu.VMEM((size + 8, size), jnp.float...  1.19 us
  transfers between devices with their start and end apart: 5, of which 2 were waited for; matrix products, arithmetic and copies ran while one was open for 0% of the time, Pallas kernels for 6%

profile of v6, /device:TPU:31, one launch (start us, length us, event | category | flops | bytes accessed | tf_op | source)
XLA Modules:
  0.0 18.6 jit_solution(8289124119250807225)
XLA Ops:
  0.6 0.7 %collective-permute-start = (f32[2,128]{1,0:T(2,128)}, f32[2,128]{1,0:T(2,128)S(1)}, u32[]{:S(2)}, u32[]{:S(2)}) collective-permute-start(f32[2,128]{1,0:T(2,128)} %read_ref.1), channel_id=1, source_target_pairs={{0,8},{4,12},{8,0},{12,4},{16,24},{20,28},{24,16},{28,20},{1,9},{5... | collective-permute-start | bytes 3080 | tf_op jit(solution)/shard_map/ppermute | solution.py:76
  1.4 0.1 collective-permute-start.1
  1.5 1.2 %prepare_window.1 = (f32[136,128]{1,0:T(8,128)S(1)}, f32[128,128]{1,0:T(8,128)S(1)}, f32[128,128]{1,0:T(8,128)S(1)}, f32[1,128]{1,0:T(1,128)S(1)}, f32[128,128]{...) custom-call(f32[2,128]{1,0:T(2,128)} %read_ref.1, ...), custom_call_target="tpu_custom_call" | custom-call | tf_op jit(solution)/shard_map/prepare_window/pallas_call | solution.py:279
  2.6 0.1 collective-permute-done.1
  2.7 0.0 collective-permute-done
  2.8 0.3 %collective-permute-start.4 = (f32[2,4,128]{2,1,0:T(4,128)S(1)}, f32[2,4,128]{2,1,0:T(4,128)S(1)}, u32[]{:S(2)}, u32[]{:S(2)}) collective-permute-start(f32[2,4,128]{2,1,0:T(4,128)S(1)} %pad_maximum_fusion), channel_id=1, source_target_pairs={{0,4},{4,0},{8,12},{12,8},{16,20},{20,16},{24,28},{28,24},{1,5},{5... | collective-permute-start | bytes 12296 | tf_op jit(solution)/shard_map/ppermute | solution.py:76
  3.1 0.2 %collective-permute-start.3 = (f32[2,4,128]{2,1,0:T(4,128)S(1)}, f32[2,4,128]{2,1,0:T(4,128)S(1)}, u32[]{:S(2)}, u32[]{:S(2)}) collective-permute-start(f32[2,4,128]{2,1,0:T(4,128)S(1)} %pad_maximum_fusion), channel_id=1, source_target_pairs={{0,16},{4,20},{8,24},{12,28},{16,0},{20,4},{24,8},{28,12},{1,17},{... | collective-permute-start | bytes 12296 | tf_op jit(solution)/shard_map/ppermute | solution.py:76
  3.3 2.2 %collective-permute-start.2 = (f32[2,4,128]{2,1,0:T(4,128)S(1)}, f32[2,4,128]{2,1,0:T(4,128)S(1)}, u32[]{:S(2)}, u32[]{:S(2)}) collective-permute-start(f32[2,4,128]{2,1,0:T(4,128)S(1)} %pad_maximum_fusion), channel_id=1, source_target_pairs={{0,20},{4,16},{8,28},{12,24},{16,4},{20,0},{24,12},{28,8},{1,21},{... | collective-permute-start | bytes 12296 | tf_op jit(solution)/shard_map/ppermute | solution.py:76
  5.5 1.2 %collective-permute-done.2 = f32[2,4,128]{2,1,0:T(4,128)S(1)} collective-permute-done((f32[2,4,128]{2,1,0:T(4,128)S(1)}, f32[2,4,128]{2,1,0:T(4,128)S(1)}, u32[]{:S(2)}, u32[]{:S(2)}) %collective-permute-start.2) | collective-permute-done | bytes 4128 | tf_op jit(solution)/shard_map/ppermute | solution.py:76
  6.7 0.0 collective-permute-done.3
  6.7 0.0 collective-permute-done.4
  6.7 11.9 %filter_window.1 = (f32[2,128]{1,0:T(2,128)}, f32[2,128,128]{2,1,0:T(8,128)}) custom-call(f32[8,4,128]{2,1,0:T(4,128)S(1)} %constant_dynamic-update-slice_fusion.steps_ref, f32[136,128]{1,0:T(8,128)S(1)} %get-tuple-element.12.start_ref, f32[128,128]{1,0:T(8,128)S(1)} %get-tuple-element.13.turned_ref, f32[128,128]{1,0:T(8,128)S(1)} %get-tuple-element.14.chosen_ref, ...), custom_call_target="tpu_custom_call" | custom-call | tf_op jit(solution)/shard_map/filter_window/pallas_call | solution.py:300
  (8 shorter events, 0.1 us)
Async XLA Ops:
  0.6 2.1 %collective-permute-start = (f32[2,128]{1,0:T(2,128)}, f32[2,128]{1,0:T(2,128)S(1)}, u32[]{:S(2)}, u32[]{:S(2)}) collective-permute-start(f32[2,128]{1,0:T(2,128)} %read_ref.1), channel_id=1, source_target_pairs={{0,8},{4,12},{8,0},{12,4},{16,24},{20,28},{24,16},{28,20},{1,9},{5... | collective-permute-start | bytes 3080 | tf_op jit(solution)/shard_map/ppermute | solution.py:76
  1.4 1.4 %collective-permute-start.1 = (s32[2,128]{1,0:T(2,128)}, s32[2,128]{1,0:T(2,128)S(1)}, u32[]{:S(2)}, u32[]{:S(2)}) collective-permute-start(s32[2,128]{1,0:T(2,128)} %mask_ref.1), channel_id=1, source_target_pairs={{0,8},{4,12},{8,0},{12,4},{16,24},{20,28},{24,16},{28,20},{1,9},{5... | collective-permute-start | bytes 3080 | tf_op jit(solution)/shard_map/ppermute | solution.py:76
  2.8 4.0 %collective-permute-start.4 = (f32[2,4,128]{2,1,0:T(4,128)S(1)}, f32[2,4,128]{2,1,0:T(4,128)S(1)}, u32[]{:S(2)}, u32[]{:S(2)}) collective-permute-start(f32[2,4,128]{2,1,0:T(4,128)S(1)} %pad_maximum_fusion), channel_id=1, source_target_pairs={{0,4},{4,0},{8,12},{12,8},{16,20},{20,16},{24,28},{28,24},{1,5},{5... | collective-permute-start | bytes 12296 | tf_op jit(solution)/shard_map/ppermute | solution.py:76
  3.1 3.6 %collective-permute-start.3 = (f32[2,4,128]{2,1,0:T(4,128)S(1)}, f32[2,4,128]{2,1,0:T(4,128)S(1)}, u32[]{:S(2)}, u32[]{:S(2)}) collective-permute-start(f32[2,4,128]{2,1,0:T(4,128)S(1)} %pad_maximum_fusion), channel_id=1, source_target_pairs={{0,16},{4,20},{8,24},{12,28},{16,0},{20,4},{24,8},{28,12},{1,17},{... | collective-permute-start | bytes 12296 | tf_op jit(solution)/shard_map/ppermute | solution.py:76
  3.3 3.4 %collective-permute-start.2 = (f32[2,4,128]{2,1,0:T(4,128)S(1)}, f32[2,4,128]{2,1,0:T(4,128)S(1)}, u32[]{:S(2)}, u32[]{:S(2)}) collective-permute-start(f32[2,4,128]{2,1,0:T(4,128)S(1)} %pad_maximum_fusion), channel_id=1, source_target_pairs={{0,20},{4,16},{8,28},{12,24},{16,4},{20,0},{24,12},{28,8},{1,21},{... | collective-permute-start | bytes 12296 | tf_op jit(solution)/shard_map/ppermute | solution.py:76

commit v7 on v6

--- a/solution.py
+++ b/solution.py
@@ -7,6 +7,7 @@
 from jax.experimental import pallas as pl
 from jax.experimental.pallas import tpu as pltpu
 from jax.sharding import PartitionSpec as P
+
 
 RADIUS = 0.6
 SERIES_BOUND = RADIUS**8
@@ -89,8 +90,12 @@
         masks = [1 << b for b in stage]
         if len(masks) == 2:
             masks = [masks[0] | masks[1], masks[1], masks[0]]
-        gathered = jnp.concatenate([gathered] + [across(gathered, m) for m in masks], 0)
-    return gathered
+        arrived = []
+        for m in masks:
+            arrived.append(across(gathered, m))
+        early = jnp.concatenate([gathered, arrived[0]], 0)
+        gathered = jnp.concatenate([gathered] + arrived, 0)
+    return early, gathered
 
 
 def prepare(
@@ -121,10 +126,11 @@
 
 def kernel(
     steps_ref, start_ref, turned_ref, chosen_ref, inv_var_ref, trans_ref, noise_ref,
-    mean_ref, prior_ref, mean_out, cov_out, prec_ref, info_ref, state_ref, check_ref, high_ref,
-    low_ref, *, stages,
+    mean_ref, prior_ref, tested_ref, mean_out, cov_out, prec_ref, info_ref, state_ref, check_ref,
+    high_ref, low_ref, *, stages, known, early,
 ):
-    parts, rows_each, width = steps_ref.shape
+    rows_each = steps_ref.shape[1]
+    parts = 1 << sum(len(stage) for stage in stages)
     per_part = rows_each // 2
     steps = parts * per_part
     size = trans_ref.shape[0]
@@ -136,14 +142,26 @@
 
     inv_var = inv_var_ref[...]
 
+    head_slot = slot_of(own, stages)
+    has_head = jnp.logical_and(head_slot < known, own > 0)
+    headway = jnp.where(has_head, per_part, 0)
+
     def place(source, carried):
-        block = steps_ref[slot_of(source ^ own, stages)]
+        if early:
+            block = steps_ref[jnp.where(has_head, head_slot, 0)]
+        else:
+            block = steps_ref[slot_of(source ^ own, stages)]
         weight = block[per_part:] * inv_var
         prec_ref[pl.ds(source * per_part, per_part), :] = weight
         info_ref[pl.ds(source * per_part, per_part), :] = weight * block[:per_part]
         return carried
 
-    lax.fori_loop(0, parts, place, 0, unroll=parts <= 8)
+    if early:
+        prec_ref[...] = jnp.zeros_like(prec_ref)
+        info_ref[...] = jnp.zeros_like(info_ref)
+        place(0, 0)
+    else:
+        lax.fori_loop(0, parts, place, 0, unroll=parts <= 8)
     chosen = chosen_ref[...].astype(jnp.bfloat16)
     left = jnp.concatenate([prec_ref[...], info_ref[...]], 0)
     summed = jnp.zeros(left.shape, jnp.float32)
@@ -155,6 +173,8 @@
     info_ref[...] = summed[steps:]
     high_ref[...], low_ref[...] = split(turned_ref[...])
     check_ref[...] = jnp.zeros_like(check_ref)
+    if not early:
+        check_ref[:per_part] = tested_ref[...]
 
     def factors(cov, mean, step):
         prec = prec_ref[pl.ds(step, 1), :]
@@ -208,7 +228,13 @@
     def body(step, carried):
         return tuple(advance(*carried, step, True, False))
 
-    cov, mean = lax.fori_loop(0, first, body, (cov, mean))
+    if early:
+        cov, mean = lax.fori_loop(0, headway, body, (cov, mean))
+        mean_out[:size] = cov
+        mean_out[size:] = mean
+        cov_out[...] = check_ref[:per_part]
+        return
+    cov, mean = lax.fori_loop(headway, first, body, (cov, mean))
     for j in range(per_part):
         moves = j + 1 < per_part
         result = advance(cov, mean, first + j, moves, True)
@@ -296,27 +322,40 @@
         observations, obs_mask, sensor_map[None], obs_var[None], transition, proc_noise,
         prior_mean[None], prior_var[None],
     )
-    gathered = gather_steps(own_rows, observations, obs_mask, stages)
+    early, gathered = gather_steps(own_rows, observations, obs_mask, stages)
+    scratch = [
+        pltpu.VMEM((steps, sensors), jnp.float32),
+        pltpu.VMEM((steps, sensors), jnp.float32),
+        pltpu.VMEM((size, size), jnp.float32),
+        pltpu.VMEM((steps, 8, size), jnp.float32),
+        pltpu.VMEM((size, size), jnp.bfloat16),
+        pltpu.VMEM((size, size), jnp.bfloat16),
+    ]
+    known = early.shape[0]
+    untested = pltpu.VMEM((steps_here, 8, size), jnp.float32)
+
+    def head(*refs):
+        kernel(*refs[:9], None, *refs[9:], stages=stages, known=known, early=True)
+
+    state, tested = pl.pallas_call(
+        head,
+        out_shape=(pltpu.VMEM((size + 8, size), jnp.float32), untested),
+        in_specs=[vmem] * 9,
+        out_specs=(vmem, vmem),
+        scratch_shapes=scratch,
+        name="filter_head",
+    )(*near(early, *prepared))
     return pl.pallas_call(
-        functools.partial(kernel, stages=stages),
+        functools.partial(kernel, stages=stages, known=known, early=False),
         out_shape=(
             jax.ShapeDtypeStruct((steps_here, size), jnp.float32),
             jax.ShapeDtypeStruct((steps_here, size, size), jnp.float32),
         ),
-        in_specs=[vmem] * 9,
+        in_specs=[vmem] * 10,
         out_specs=(vmem, vmem),
-        scratch_shapes=[
-            pltpu.VMEM((steps, sensors), jnp.float32),
-            pltpu.VMEM((steps, sensors), jnp.float32),
-            pltpu.VMEM((size, size), jnp.float32),
-            pltpu.VMEM((steps, 8, size), jnp.float32),
-            pltpu.VMEM((size, size), jnp.bfloat16),
-            pltpu.VMEM((size, size), jnp.bfloat16),
-        ],
+        scratch_shapes=scratch,
         name="filter_window",
-    )(
-        *near(gathered, *prepared)
-    )
+    )(*near(gathered, state, *prepared[1:], tested))
 
 
 def solution(mesh):

time: 18.8 us -> 19 us (1.011)
    pallas_call x1 -> x2, Pallas kernels: 11.9 us -> 12.1 us  [the longest x1 10.5 us: local(): pl.pallas_call(functools.partial(kernel, stages=stages, known=known, earl...]
  transfers between devices with their start and end apart: 5 -> 5, of which waited for: 2 -> 2; matrix products, arithmetic and copies ran while one was open for 0% -> 0% of each run, Pallas kernels for 6% -> 14%
where the time goes in v7:
time: 19 us; the launch traced here: 18.8 us
  Pallas kernels  13.2 us (69%)
  starting transfers between devices  3.53 us (19%)
  waiting for transfers between devices  1.3 us (7%)
  between operations  0.68 us (4%)
    pallas_call x1, Pallas kernels, local(): pl.pallas_call(functools.partial(kernel, stages=stages, known=known, earl...  10.5 us
    ppermute x5, starting transfers between devices, across(): return lax.ppermute(value, TIME_AXES, [(i, i ^ mask) for i in range(parts)])  3.53 us
    pallas_call x1, Pallas kernels, local(): pl.pallas_call(head, out_shape=(pltpu.VMEM((size + 8, size), jnp.float32)...  1.53 us
    ppermute x5, waiting for transfers between devices, across(): return lax.ppermute(value, TIME_AXES, [(i, i ^ mask) for i in range(parts)])  1.3 us
    pallas_call x1, Pallas kernels, local(): pl.pallas_call(prepare, out_shape=(pltpu.VMEM((size + 8, size), jnp.float...  1.19 us
  transfers between devices with their start and end apart: 5, of which 2 were waited for; matrix products, arithmetic and copies ran while one was open for 0% of the time, Pallas kernels for 14%

profile of v7, /device:TPU:31, one launch (start us, length us, event | category | flops | bytes accessed | tf_op | source)
XLA Modules:
  0.0 18.8 jit_solution(11864960697898078310)
XLA Ops:
  0.6 0.7 %collective-permute-start = (f32[2,128]{1,0:T(2,128)}, f32[2,128]{1,0:T(2,128)S(1)}, u32[]{:S(2)}, u32[]{:S(2)}) collective-permute-start(f32[2,128]{1,0:T(2,128)} %read_ref.1), channel_id=1, source_target_pairs={{0,8},{4,12},{8,0},{12,4},{16,24},{20,28},{24,16},{28,20},{1,9},{5... | collective-permute-start | bytes 3080 | tf_op jit(solution)/shard_map/ppermute | solution.py:77
  1.4 0.1 collective-permute-start.1
  1.5 1.2 %prepare_window.1 = (f32[136,128]{1,0:T(8,128)S(1)}, f32[128,128]{1,0:T(8,128)S(1)}, f32[128,128]{1,0:T(8,128)S(1)}, f32[1,128]{1,0:T(1,128)S(1)}, f32[128,128]{...) custom-call(f32[2,128]{1,0:T(2,128)} %read_ref.1, ...), custom_call_target="tpu_custom_call" | custom-call | tf_op jit(solution)/shard_map/prepare_window/pallas_call | solution.py:305
  2.6 0.1 collective-permute-done.1
  2.7 0.0 collective-permute-done
  2.8 0.3 %collective-permute-start.4 = (f32[2,4,128]{2,1,0:T(4,128)S(1)}, f32[2,4,128]{2,1,0:T(4,128)S(1)}, u32[]{:S(2)}, u32[]{:S(2)}) collective-permute-start(f32[2,4,128]{2,1,0:T(4,128)S(1)} %pad_maximum_fusion.1), channel_id=1, source_target_pairs={{0,4},{4,0},{8,12},{12,8},{16,20},{20,16},{24,28},{28,24},{1,5},{5... | collective-permute-start | bytes 12296 | tf_op jit(solution)/shard_map/ppermute | solution.py:77
  3.1 0.2 %collective-permute-start.3 = (f32[2,4,128]{2,1,0:T(4,128)S(1)}, f32[2,4,128]{2,1,0:T(4,128)S(1)}, u32[]{:S(2)}, u32[]{:S(2)}) collective-permute-start(f32[2,4,128]{2,1,0:T(4,128)S(1)} %pad_maximum_fusion.1), channel_id=1, source_target_pairs={{0,16},{4,20},{8,24},{12,28},{16,0},{20,4},{24,8},{28,12},{1,17},{... | collective-permute-start | bytes 12296 | tf_op jit(solution)/shard_map/ppermute | solution.py:77
  3.3 2.2 %collective-permute-start.2 = (f32[2,4,128]{2,1,0:T(4,128)S(1)}, f32[2,4,128]{2,1,0:T(4,128)S(1)}, u32[]{:S(2)}, u32[]{:S(2)}) collective-permute-start(f32[2,4,128]{2,1,0:T(4,128)S(1)} %pad_maximum_fusion.1), channel_id=1, source_target_pairs={{0,20},{4,16},{8,28},{12,24},{16,4},{20,0},{24,12},{28,8},{1,21},{... | collective-permute-start | bytes 12296 | tf_op jit(solution)/shard_map/ppermute | solution.py:77
  5.5 1.2 %collective-permute-done.2 = f32[2,4,128]{2,1,0:T(4,128)S(1)} collective-permute-done((f32[2,4,128]{2,1,0:T(4,128)S(1)}, f32[2,4,128]{2,1,0:T(4,128)S(1)}, u32[]{:S(2)}, u32[]{:S(2)}) %collective-permute-start.2) | collective-permute-done | bytes 4128 | tf_op jit(solution)/shard_map/ppermute | solution.py:77
  6.7 0.0 collective-permute-done.3
  6.7 1.5 %filter_head.1 = (f32[136,128]{1,0:T(8,128)S(1)}, f32[2,8,128]{2,1,0:T(8,128)S(1)}) custom-call(f32[4,4,128]{2,1,0:T(4,128)S(1)} %pad_maximum_fusion.refs_0_, f32[136,128]{1,0:T(8,128)S(1)} %get-tuple-element.14.refs_1_, f32[128,128]{1,0:T(8,128)S(1)} %get-tuple-element.15.refs_2_.turned_ref, f32[128,128]{1,0:T(8,128)S(1)} %get-tuple-element.16.refs_3_.chosen_ref, ...), custom_call_target="tpu_custom_call" | custom-call | tf_op jit(solution)/shard_map/filter_head/pallas_call | solution.py:340
  8.3 0.0 collective-permute-done.4
  8.3 10.5 %filter_window.1 = (f32[2,128]{1,0:T(2,128)}, f32[2,128,128]{2,1,0:T(8,128)}) custom-call(f32[8,4,128]{2,1,0:T(4,128)S(1)} %constant_dynamic-update-slice_fusion.steps_ref, f32[136,128]{1,0:T(8,128)S(1)} %get-tuple-element.22.start_ref, f32[128,128]{1,0:T(8,128)S(1)} %get-tuple-element.15.refs_2_.turned_ref, ...), custom_call_target="tpu_custom_call" | custom-call | tf_op jit(solution)/shard_map/filter_window/pallas_call | solution.py:348
  (9 shorter events, 0.1 us)
Async XLA Ops:
  0.6 2.1 %collective-permute-start = (f32[2,128]{1,0:T(2,128)}, f32[2,128]{1,0:T(2,128)S(1)}, u32[]{:S(2)}, u32[]{:S(2)}) collective-permute-start(f32[2,128]{1,0:T(2,128)} %read_ref.1), channel_id=1, source_target_pairs={{0,8},{4,12},{8,0},{12,4},{16,24},{20,28},{24,16},{28,20},{1,9},{5... | collective-permute-start | bytes 3080 | tf_op jit(solution)/shard_map/ppermute | solution.py:77
  1.4 1.4 %collective-permute-start.1 = (s32[2,128]{1,0:T(2,128)}, s32[2,128]{1,0:T(2,128)S(1)}, u32[]{:S(2)}, u32[]{:S(2)}) collective-permute-start(s32[2,128]{1,0:T(2,128)} %mask_ref.1), channel_id=1, source_target_pairs={{0,8},{4,12},{8,0},{12,4},{16,24},{20,28},{24,16},{28,20},{1,9},{5... | collective-permute-start | bytes 3080 | tf_op jit(solution)/shard_map/ppermute | solution.py:77
  2.8 5.5 %collective-permute-start.4 = (f32[2,4,128]{2,1,0:T(4,128)S(1)}, f32[2,4,128]{2,1,0:T(4,128)S(1)}, u32[]{:S(2)}, u32[]{:S(2)}) collective-permute-start(f32[2,4,128]{2,1,0:T(4,128)S(1)} %pad_maximum_fusion.1), channel_id=1, source_target_pairs={{0,4},{4,0},{8,12},{12,8},{16,20},{20,16},{24,28},{28,24},{1,5},{5... | collective-permute-start | bytes 12296 | tf_op jit(solution)/shard_map/ppermute | solution.py:77
  3.1 3.6 %collective-permute-start.3 = (f32[2,4,128]{2,1,0:T(4,128)S(1)}, f32[2,4,128]{2,1,0:T(4,128)S(1)}, u32[]{:S(2)}, u32[]{:S(2)}) collective-permute-start(f32[2,4,128]{2,1,0:T(4,128)S(1)} %pad_maximum_fusion.1), channel_id=1, source_target_pairs={{0,16},{4,20},{8,24},{12,28},{16,0},{20,4},{24,8},{28,12},{1,17},{... | collective-permute-start | bytes 12296 | tf_op jit(solution)/shard_map/ppermute | solution.py:77
  3.3 3.4 %collective-permute-start.2 = (f32[2,4,128]{2,1,0:T(4,128)S(1)}, f32[2,4,128]{2,1,0:T(4,128)S(1)}, u32[]{:S(2)}, u32[]{:S(2)}) collective-permute-start(f32[2,4,128]{2,1,0:T(4,128)S(1)} %pad_maximum_fusion.1), channel_id=1, source_target_pairs={{0,20},{4,16},{8,28},{12,24},{16,4},{20,0},{24,12},{28,8},{1,21},{... | collective-permute-start | bytes 12296 | tf_op jit(solution)/shard_map/ppermute | solution.py:77

commit v8 on v7

--- a/solution.py
+++ b/solution.py
@@ -190,8 +190,8 @@
 
     def advance(cov, mean, step, move, outs):
         shrink, series, push = factors(cov, mean, step)
+        whole_series = series
         series = split(series)
-        pow2 = mul(series, series)
         lefts = []
         rights = []
         if move:
@@ -202,6 +202,12 @@
             lefts.append(jnp.where(on_diag, jnp.broadcast_to(shrink * whole, (size, size)), 0.0))
             rights.append(cov)
         lefts[-1] = jnp.concatenate([lefts[-1], push * whole], 0)
+        stacked = mul(split(jnp.concatenate([whole_series] + lefts, 0)), series)
+        pow2 = stacked[:size]
+        lowered = [stacked[size:]]
+        if len(lefts) == 2:
+            lowered = [stacked[size : 2 * size], stacked[2 * size :]]
+        lefts = [left - low for left, low in zip(lefts, lowered)]
         pow2_split = split(pow2)
         pow4 = jnp.dot(pow2_split[0], pow2_split[0], preferred_element_type=jnp.float32)
         check_ref[step] = jnp.sum((pow4 * pow4).reshape(size // 8, 8, size), axis=0)
@@ -209,7 +215,6 @@
         even_right = split(pow4 + pow2 * narrow[0])
         done = []
         for left in lefts:
-            left = left - mul(split(left), series)
             left = left * square + mul(split(left), pow2_split)
             done.append(split(left * wide[1] + mul(split(left), even_left)))
         rights = [split(right * narrow[1] + mul(even_right, split(right))) for right in rights]

time: 19 us -> 19.1 us (level)
  Pallas kernels: 13.2 us -> 13.4 us
where the time goes in v8:
time: 19.1 us; the launch traced here: 18.9 us
  Pallas kernels  13.4 us (70%)
  starting transfers between devices  3.53 us (18%)
  waiting for transfers between devices  1.3 us (7%)
  between operations  0.68 us (4%)
    pallas_call x1, Pallas kernels, local(): pl.pallas_call(functools.partial(kernel, stages=stages, known=known, earl...  10.6 us
    ppermute x5, starting transfers between devices, across(): return lax.ppermute(value, TIME_AXES, [(i, i ^ mask) for i in range(parts)])  3.53 us
    pallas_call x1, Pallas kernels, local(): pl.pallas_call(head, out_shape=(pltpu.VMEM((size + 8, size), jnp.float32)...  1.54 us
    ppermute x5, waiting for transfers between devices, across(): return lax.ppermute(value, TIME_AXES, [(i, i ^ mask) for i in range(parts)])  1.3 us
    pallas_call x1, Pallas kernels, local(): pl.pallas_call(prepare, out_shape=(pltpu.VMEM((size + 8, size), jnp.float...  1.19 us
  transfers between devices with their start and end apart: 5, of which 2 were waited for; matrix products, arithmetic and copies ran while one was open for 0% of the time, Pallas kernels for 14%

profile of v8, /device:TPU:31, one launch (start us, length us, event | category | flops | bytes accessed | tf_op | source)
XLA Modules:
  0.0 18.9 jit_solution(3341636625144375636)
XLA Ops:
  0.6 0.7 %collective-permute-start = (f32[2,128]{1,0:T(2,128)}, f32[2,128]{1,0:T(2,128)S(1)}, u32[]{:S(2)}, u32[]{:S(2)}) collective-permute-start(f32[2,128]{1,0:T(2,128)} %read_ref.1), channel_id=1, source_target_pairs={{0,8},{4,12},{8,0},{12,4},{16,24},{20,28},{24,16},{28,20},{1,9},{5... | collective-permute-start | bytes 3080 | tf_op jit(solution)/shard_map/ppermute | solution.py:77
  1.4 0.1 collective-permute-start.1
  1.5 1.2 %prepare_window.1 = (f32[136,128]{1,0:T(8,128)S(1)}, f32[128,128]{1,0:T(8,128)S(1)}, f32[128,128]{1,0:T(8,128)S(1)}, f32[1,128]{1,0:T(1,128)S(1)}, f32[128,128]{...) custom-call(f32[2,128]{1,0:T(2,128)} %read_ref.1, ...), custom_call_target="tpu_custom_call" | custom-call | tf_op jit(solution)/shard_map/prepare_window/pallas_call | solution.py:310
  2.6 0.1 collective-permute-done.1
  2.7 0.0 collective-permute-done
  2.8 0.3 %collective-permute-start.4 = (f32[2,4,128]{2,1,0:T(4,128)S(1)}, f32[2,4,128]{2,1,0:T(4,128)S(1)}, u32[]{:S(2)}, u32[]{:S(2)}) collective-permute-start(f32[2,4,128]{2,1,0:T(4,128)S(1)} %pad_maximum_fusion.1), channel_id=1, source_target_pairs={{0,4},{4,0},{8,12},{12,8},{16,20},{20,16},{24,28},{28,24},{1,5},{5... | collective-permute-start | bytes 12296 | tf_op jit(solution)/shard_map/ppermute | solution.py:77
  3.1 0.2 %collective-permute-start.3 = (f32[2,4,128]{2,1,0:T(4,128)S(1)}, f32[2,4,128]{2,1,0:T(4,128)S(1)}, u32[]{:S(2)}, u32[]{:S(2)}) collective-permute-start(f32[2,4,128]{2,1,0:T(4,128)S(1)} %pad_maximum_fusion.1), channel_id=1, source_target_pairs={{0,16},{4,20},{8,24},{12,28},{16,0},{20,4},{24,8},{28,12},{1,17},{... | collective-permute-start | bytes 12296 | tf_op jit(solution)/shard_map/ppermute | solution.py:77
  3.3 2.2 %collective-permute-start.2 = (f32[2,4,128]{2,1,0:T(4,128)S(1)}, f32[2,4,128]{2,1,0:T(4,128)S(1)}, u32[]{:S(2)}, u32[]{:S(2)}) collective-permute-start(f32[2,4,128]{2,1,0:T(4,128)S(1)} %pad_maximum_fusion.1), channel_id=1, source_target_pairs={{0,20},{4,16},{8,28},{12,24},{16,4},{20,0},{24,12},{28,8},{1,21},{... | collective-permute-start | bytes 12296 | tf_op jit(solution)/shard_map/ppermute | solution.py:77
  5.5 1.2 %collective-permute-done.2 = f32[2,4,128]{2,1,0:T(4,128)S(1)} collective-permute-done((f32[2,4,128]{2,1,0:T(4,128)S(1)}, f32[2,4,128]{2,1,0:T(4,128)S(1)}, u32[]{:S(2)}, u32[]{:S(2)}) %collective-permute-start.2) | collective-permute-done | bytes 4128 | tf_op jit(solution)/shard_map/ppermute | solution.py:77
  6.7 0.0 collective-permute-done.3
  6.7 1.5 %filter_head.1 = (f32[136,128]{1,0:T(8,128)S(1)}, f32[2,8,128]{2,1,0:T(8,128)S(1)}) custom-call(f32[4,4,128]{2,1,0:T(4,128)S(1)} %pad_maximum_fusion.refs_0_, f32[136,128]{1,0:T(8,128)S(1)} %get-tuple-element.14.refs_1_, f32[128,128]{1,0:T(8,128)S(1)} %get-tuple-element.15.refs_2_.turned_ref, f32[128,128]{1,0:T(8,128)S(1)} %get-tuple-element.16.refs_3_.chosen_ref, ...), custom_call_target="tpu_custom_call" | custom-call | tf_op jit(solution)/shard_map/filter_head/pallas_call | solution.py:345
  8.3 0.0 collective-permute-done.4
  8.3 10.6 %filter_window.1 = (f32[2,128]{1,0:T(2,128)}, f32[2,128,128]{2,1,0:T(8,128)}) custom-call(f32[8,4,128]{2,1,0:T(4,128)S(1)} %constant_dynamic-update-slice_fusion.steps_ref, f32[136,128]{1,0:T(8,128)S(1)} %get-tuple-element.22.start_ref, f32[128,128]{1,0:T(8,128)S(1)} %get-tuple-element.15.refs_2_.turned_ref, ...), custom_call_target="tpu_custom_call" | custom-call | tf_op jit(solution)/shard_map/filter_window/pallas_call | solution.py:353
  (9 shorter events, 0.1 us)
Async XLA Ops:
  0.6 2.1 %collective-permute-start = (f32[2,128]{1,0:T(2,128)}, f32[2,128]{1,0:T(2,128)S(1)}, u32[]{:S(2)}, u32[]{:S(2)}) collective-permute-start(f32[2,128]{1,0:T(2,128)} %read_ref.1), channel_id=1, source_target_pairs={{0,8},{4,12},{8,0},{12,4},{16,24},{20,28},{24,16},{28,20},{1,9},{5... | collective-permute-start | bytes 3080 | tf_op jit(solution)/shard_map/ppermute | solution.py:77
  1.4 1.4 %collective-permute-start.1 = (s32[2,128]{1,0:T(2,128)}, s32[2,128]{1,0:T(2,128)S(1)}, u32[]{:S(2)}, u32[]{:S(2)}) collective-permute-start(s32[2,128]{1,0:T(2,128)} %mask_ref.1), channel_id=1, source_target_pairs={{0,8},{4,12},{8,0},{12,4},{16,24},{20,28},{24,16},{28,20},{1,9},{5... | collective-permute-start | bytes 3080 | tf_op jit(solution)/shard_map/ppermute | solution.py:77
  2.8 5.5 %collective-permute-start.4 = (f32[2,4,128]{2,1,0:T(4,128)S(1)}, f32[2,4,128]{2,1,0:T(4,128)S(1)}, u32[]{:S(2)}, u32[]{:S(2)}) collective-permute-start(f32[2,4,128]{2,1,0:T(4,128)S(1)} %pad_maximum_fusion.1), channel_id=1, source_target_pairs={{0,4},{4,0},{8,12},{12,8},{16,20},{20,16},{24,28},{28,24},{1,5},{5... | collective-permute-start | bytes 12296 | tf_op jit(solution)/shard_map/ppermute | solution.py:77
  3.1 3.6 %collective-permute-start.3 = (f32[2,4,128]{2,1,0:T(4,128)S(1)}, f32[2,4,128]{2,1,0:T(4,128)S(1)}, u32[]{:S(2)}, u32[]{:S(2)}) collective-permute-start(f32[2,4,128]{2,1,0:T(4,128)S(1)} %pad_maximum_fusion.1), channel_id=1, source_target_pairs={{0,16},{4,20},{8,24},{12,28},{16,0},{20,4},{24,8},{28,12},{1,17},{... | collective-permute-start | bytes 12296 | tf_op jit(solution)/shard_map/ppermute | solution.py:77
  3.3 3.4 %collective-permute-start.2 = (f32[2,4,128]{2,1,0:T(4,128)S(1)}, f32[2,4,128]{2,1,0:T(4,128)S(1)}, u32[]{:S(2)}, u32[]{:S(2)}) collective-permute-start(f32[2,4,128]{2,1,0:T(4,128)S(1)} %pad_maximum_fusion.1), channel_id=1, source_target_pairs={{0,20},{4,16},{8,28},{12,24},{16,4},{20,0},{24,12},{28,8},{1,21},{... | collective-permute-start | bytes 12296 | tf_op jit(solution)/shard_map/ppermute | solution.py:77

commit v9 on v8

--- a/solution.py
+++ b/solution.py
@@ -116,7 +116,7 @@
     start_ref[size:] = rows[size:]
     components = lax.broadcasted_iota(jnp.int32, (size, sensors), 0)
     chosen = (components == map_ref[...]).astype(jnp.float32)
-    chosen_ref[...] = chosen.T
+    chosen_ref[...] = chosen.T.astype(jnp.bfloat16)
     inv_var_ref[...] = 1.0 / var_ref[...]
     trans_out[...] = trans
     noise_out[...] = noise_ref[...]
@@ -162,7 +162,7 @@
         place(0, 0)
     else:
         lax.fori_loop(0, parts, place, 0, unroll=parts <= 8)
-    chosen = chosen_ref[...].astype(jnp.bfloat16)
+    chosen = chosen_ref[...]
     left = jnp.concatenate([prec_ref[...], info_ref[...]], 0)
     summed = jnp.zeros(left.shape, jnp.float32)
     for _ in range(3):
@@ -312,7 +312,7 @@
         out_shape=(
             pltpu.VMEM((size + 8, size), jnp.float32),
             pltpu.VMEM((size, size), jnp.float32),
-            pltpu.VMEM((sensors, size), jnp.float32),
+            pltpu.VMEM((sensors, size), jnp.bfloat16),
             pltpu.VMEM((1, sensors), jnp.float32),
             pltpu.VMEM((size, size), jnp.float32),
             pltpu.VMEM((size, size), jnp.float32),

time: 19.1 us -> 19.1 us (level)
  no operation moved by 1% of the time
where the time goes in v9:
time: 19.1 us; the launch traced here: 18.9 us
  Pallas kernels  13.4 us (70%)
  starting transfers between devices  3.53 us (18%)
  waiting for transfers between devices  1.3 us (7%)
  between operations  0.69 us (4%)
    pallas_call x1, Pallas kernels, local(): pl.pallas_call(functools.partial(kernel, stages=stages, known=known, earl...  10.6 us
    ppermute x5, starting transfers between devices, across(): return lax.ppermute(value, TIME_AXES, [(i, i ^ mask) for i in range(parts)])  3.53 us
    pallas_call x1, Pallas kernels, local(): pl.pallas_call(head, out_shape=(pltpu.VMEM((size + 8, size), jnp.float32)...  1.54 us
    ppermute x5, waiting for transfers between devices, across(): return lax.ppermute(value, TIME_AXES, [(i, i ^ mask) for i in range(parts)])  1.3 us
    pallas_call x1, Pallas kernels, local(): pl.pallas_call(prepare, out_shape=(pltpu.VMEM((size + 8, size), jnp.float...  1.19 us
  transfers between devices with their start and end apart: 5, of which 2 were waited for; matrix products, arithmetic and copies ran while one was open for 0% of the time, Pallas kernels for 14%

profile of v9, /device:TPU:31, one launch (start us, length us, event | category | flops | bytes accessed | tf_op | source)
XLA Modules:
  0.0 18.9 jit_solution(9940147770545829064)
XLA Ops:
  0.6 0.7 %collective-permute-start = (f32[2,128]{1,0:T(2,128)}, f32[2,128]{1,0:T(2,128)S(1)}, u32[]{:S(2)}, u32[]{:S(2)}) collective-permute-start(f32[2,128]{1,0:T(2,128)} %read_ref.1), channel_id=1, source_target_pairs={{0,8},{4,12},{8,0},{12,4},{16,24},{20,28},{24,16},{28,20},{1,9},{5... | collective-permute-start | bytes 3080 | tf_op jit(solution)/shard_map/ppermute | solution.py:77
  1.4 0.1 collective-permute-start.1
  1.5 1.2 %prepare_window.1 = (f32[136,128]{1,0:T(8,128)S(1)}, f32[128,128]{1,0:T(8,128)S(1)}, bf16[128,128]{1,0:T(8,128)(2,1)S(1)}, f32[1,128]{1,0:T(1,128)S(1)}, f32[128...) custom-call(f32[2,128]{1,0:T(2,128)} %read_ref.1, ...), custom_call_target="tpu_custom_call" | custom-call | tf_op jit(solution)/shard_map/prepare_window/pallas_call | solution.py:310
  2.6 0.1 collective-permute-done.1
  2.7 0.0 collective-permute-done
  2.8 0.3 %collective-permute-start.4 = (f32[2,4,128]{2,1,0:T(4,128)S(1)}, f32[2,4,128]{2,1,0:T(4,128)S(1)}, u32[]{:S(2)}, u32[]{:S(2)}) collective-permute-start(f32[2,4,128]{2,1,0:T(4,128)S(1)} %pad_maximum_fusion.1), channel_id=1, source_target_pairs={{0,4},{4,0},{8,12},{12,8},{16,20},{20,16},{24,28},{28,24},{1,5},{5... | collective-permute-start | bytes 12296 | tf_op jit(solution)/shard_map/ppermute | solution.py:77
  3.1 0.2 %collective-permute-start.3 = (f32[2,4,128]{2,1,0:T(4,128)S(1)}, f32[2,4,128]{2,1,0:T(4,128)S(1)}, u32[]{:S(2)}, u32[]{:S(2)}) collective-permute-start(f32[2,4,128]{2,1,0:T(4,128)S(1)} %pad_maximum_fusion.1), channel_id=1, source_target_pairs={{0,16},{4,20},{8,24},{12,28},{16,0},{20,4},{24,8},{28,12},{1,17},{... | collective-permute-start | bytes 12296 | tf_op jit(solution)/shard_map/ppermute | solution.py:77
  3.3 2.2 %collective-permute-start.2 = (f32[2,4,128]{2,1,0:T(4,128)S(1)}, f32[2,4,128]{2,1,0:T(4,128)S(1)}, u32[]{:S(2)}, u32[]{:S(2)}) collective-permute-start(f32[2,4,128]{2,1,0:T(4,128)S(1)} %pad_maximum_fusion.1), channel_id=1, source_target_pairs={{0,20},{4,16},{8,28},{12,24},{16,4},{20,0},{24,12},{28,8},{1,21},{... | collective-permute-start | bytes 12296 | tf_op jit(solution)/shard_map/ppermute | solution.py:77
  5.5 1.2 %collective-permute-done.2 = f32[2,4,128]{2,1,0:T(4,128)S(1)} collective-permute-done((f32[2,4,128]{2,1,0:T(4,128)S(1)}, f32[2,4,128]{2,1,0:T(4,128)S(1)}, u32[]{:S(2)}, u32[]{:S(2)}) %collective-permute-start.2) | collective-permute-done | bytes 4128 | tf_op jit(solution)/shard_map/ppermute | solution.py:77
  6.7 0.0 collective-permute-done.3
  6.7 1.5 %filter_head.1 = (f32[136,128]{1,0:T(8,128)S(1)}, f32[2,8,128]{2,1,0:T(8,128)S(1)}) custom-call(f32[4,4,128]{2,1,0:T(4,128)S(1)} %pad_maximum_fusion.refs_0_, f32[136,128]{1,0:T(8,128)S(1)} %get-tuple-element.14.refs_1_, f32[128,128]{1,0:T(8,128)S(1)} %get-tuple-element.15.refs_2_.turned_ref, bf16[128,128]{1,0:T(8,128)(2,1)S(1)} %get-tuple-element.16.refs_3_.chosen_ref, ...), custom_call_target="tpu_custom_call" | custom-call | tf_op jit(solution)/shard_map/filter_head/pallas_call | solution.py:345
  8.3 0.0 collective-permute-done.4
  8.3 10.6 %filter_window.1 = (f32[2,128]{1,0:T(2,128)}, f32[2,128,128]{2,1,0:T(8,128)}) custom-call(f32[8,4,128]{2,1,0:T(4,128)S(1)} %constant_dynamic-update-slice_fusion.steps_ref, f32[136,128]{1,0:T(8,128)S(1)} %get-tuple-element.22.start_ref, f32[128,128]{1,0:T(8,128)S(1)} %get-tuple-element.15.refs_2_.turned_ref, ...), custom_call_target="tpu_custom_call" | custom-call | tf_op jit(solution)/shard_map/filter_window/pallas_call | solution.py:353
  (9 shorter events, 0.1 us)
Async XLA Ops:
  0.6 2.1 %collective-permute-start = (f32[2,128]{1,0:T(2,128)}, f32[2,128]{1,0:T(2,128)S(1)}, u32[]{:S(2)}, u32[]{:S(2)}) collective-permute-start(f32[2,128]{1,0:T(2,128)} %read_ref.1), channel_id=1, source_target_pairs={{0,8},{4,12},{8,0},{12,4},{16,24},{20,28},{24,16},{28,20},{1,9},{5... | collective-permute-start | bytes 3080 | tf_op jit(solution)/shard_map/ppermute | solution.py:77
  1.4 1.4 %collective-permute-start.1 = (s32[2,128]{1,0:T(2,128)}, s32[2,128]{1,0:T(2,128)S(1)}, u32[]{:S(2)}, u32[]{:S(2)}) collective-permute-start(s32[2,128]{1,0:T(2,128)} %mask_ref.1), channel_id=1, source_target_pairs={{0,8},{4,12},{8,0},{12,4},{16,24},{20,28},{24,16},{28,20},{1,9},{5... | collective-permute-start | bytes 3080 | tf_op jit(solution)/shard_map/ppermute | solution.py:77
  2.8 5.5 %collective-permute-start.4 = (f32[2,4,128]{2,1,0:T(4,128)S(1)}, f32[2,4,128]{2,1,0:T(4,128)S(1)}, u32[]{:S(2)}, u32[]{:S(2)}) collective-permute-start(f32[2,4,128]{2,1,0:T(4,128)S(1)} %pad_maximum_fusion.1), channel_id=1, source_target_pairs={{0,4},{4,0},{8,12},{12,8},{16,20},{20,16},{24,28},{28,24},{1,5},{5... | collective-permute-start | bytes 12296 | tf_op jit(solution)/shard_map/ppermute | solution.py:77
  3.1 3.6 %collective-permute-start.3 = (f32[2,4,128]{2,1,0:T(4,128)S(1)}, f32[2,4,128]{2,1,0:T(4,128)S(1)}, u32[]{:S(2)}, u32[]{:S(2)}) collective-permute-start(f32[2,4,128]{2,1,0:T(4,128)S(1)} %pad_maximum_fusion.1), channel_id=1, source_target_pairs={{0,16},{4,20},{8,24},{12,28},{16,0},{20,4},{24,8},{28,12},{1,17},{... | collective-permute-start | bytes 12296 | tf_op jit(solution)/shard_map/ppermute | solution.py:77
  3.3 3.4 %collective-permute-start.2 = (f32[2,4,128]{2,1,0:T(4,128)S(1)}, f32[2,4,128]{2,1,0:T(4,128)S(1)}, u32[]{:S(2)}, u32[]{:S(2)}) collective-permute-start(f32[2,4,128]{2,1,0:T(4,128)S(1)} %pad_maximum_fusion.1), channel_id=1, source_target_pairs={{0,20},{4,16},{8,28},{12,24},{16,4},{20,0},{24,12},{28,8},{1,21},{... | collective-permute-start | bytes 12296 | tf_op jit(solution)/shard_map/ppermute | solution.py:77
